TPU v7x, 256 devices: a whole 4x4x8 slice. The times are simulated.
256 devices in a mesh: dp: 8 (over z_lo, core), seq: 16 (over x, y), mp: 2 (over z_hi).
Axes of the slice: x: 4, y: 4, z: 8 (z_hi: 2, z_lo: 4; z = z_hi * 4 + z_lo), core: 2. Of those that a mesh axis runs over, the one named last changes fastest.
Arguments:
- features: bfloat16 [8, 8192, 1408], P('dp', ('seq', 'mp')), may hold values from -6 to 6
- conv_weight: bfloat16 [5, 1408, 1536], P(None, ('seq', 'mp')), may hold values from -0.0625 to 0.0625
- norm_gain: float32 [1536], replicated, may hold values from 0.25 to 1.75
- query_weight: bfloat16 [1536, 1024], replicated, may hold values from -0.15625 to 0.15625
- keyval_weight: bfloat16 [1536, 320], replicated, may hold values from -0.15625 to 0.15625
- head_scale: float32 [8], replicated, may hold values from 0.5 to 24
- output_weight: bfloat16 [1536, 1536], replicated, may hold values from -0.15625 to 0.15625
- pair_weight: bfloat16 [1536, 256], replicated, may hold values from -0.625 to 0.625
- pair_input: bfloat16 [8, 256, 256, 128], P('dp', ('seq', 'mp')), may hold values from -6 to 6
- flip_weight: bfloat16 [128, 128], replicated, may hold values from -0.5 to 0.5
- pair_cotangent: bfloat16 [8, 256, 256, 128], P('dp', ('seq', 'mp')), may hold values from -0.0234375 to 0.0234375
Outputs:
- block_out: bfloat16 [8, 4096, 1536], P('dp', ('seq', 'mp'))
- pair_out: bfloat16 [8, 256, 256, 128], P('dp', ('seq', 'mp'))
- grad_flip: float32 [128, 128], replicated
All inputs are finite; a program needn't handle non-finite values.
Results may differ from a plain program's by a relative error of at most 0.011.
Values may be sent and summed in bfloat16 or wider, within the bound.
A program may use at most 192 MiB of HBM per device.

v0:
```python
import math

import jax
import jax.numpy as jnp
from jax import lax
from jax.sharding import PartitionSpec as P

PAIR_POOL = 16


norm_eps = 1e-06
logit_cap = 50.0


def padded_2(shard, sides, width):
    for axis, dim in sides:
        devices, length = (lax.axis_size(axis), shard.shape[dim])
        up = [(i, (i + 1) % devices) for i in range(devices - 1)]
        down = [(j, i) for i, j in up]
        last = lax.slice_in_dim(shard, length - width, length, axis=dim)
        initial = lax.slice_in_dim(shard, 0, width, axis=dim)
        before = lax.ppermute(last, axis, up)
        after = lax.ppermute(initial, axis, down)
        shard = jnp.concatenate([before, shard, after], axis=dim)
    return shard


def root_norm(values_in):
    return values_in * lax.rsqrt(jnp.mean(values_in * values_in, axis=-1, keepdims=True) + norm_eps)


def prepare(raw):
    return jax.nn.gelu(root_norm(raw.astype(jnp.float32)), approximate=False).astype(jnp.bfloat16)


def tap_sum(source, out_rows, tap_count, running, filter_rows):
    for lag_index in range(tap_count):
        running = running + jnp.dot(
            source[lag_index : lag_index + out_rows],
            filter_rows[lag_index],
            preferred_element_type=jnp.float32,
        )
    return running


def per_device(
    features,
    conv_weight,
    norm_gain,
    query_weight,
    keyval_weight,
    head_scale,
    output_weight,
    pair_weight,
    pair_input,
    flip_weight,
    pair_cotangent,
):
    fine_rows = features.shape[1]
    coarse_rows = fine_rows // 2
    in_channels = features.shape[2]
    model_dim = output_weight.shape[1]
    head_count = head_scale.shape[0]
    key_dim = query_weight.shape[1] // head_count
    pair_dim = flip_weight.shape[0]
    tap_count = conv_weight.shape[0]
    margin = tap_count // 2
    padded = padded_2(features, ((("seq", "mp"), 1),), margin)
    prepared = prepare(padded[0])
    starting = jnp.zeros((fine_rows, model_dim), jnp.float32)
    conv_sum = tap_sum(
        prepared,
        fine_rows,
        tap_count,
        starting,
        lax.all_gather(conv_weight, ("seq", "mp"), axis=1, tiled=True),
    )
    skipped = jnp.pad(features[0].astype(jnp.float32), ((0, 0), (0, model_dim - in_channels)))
    encoded = jnp.max((conv_sum + skipped).reshape(coarse_rows, 2, model_dim), axis=1).astype(
        jnp.bfloat16
    )
    widened = encoded.astype(jnp.float32)
    normed = (root_norm(widened) * norm_gain).astype(jnp.bfloat16)
    scale_row = jnp.repeat(head_scale, key_dim) / math.sqrt(key_dim)
    queries = (
        jnp.dot(normed, query_weight, preferred_element_type=jnp.float32) * scale_row
    ).astype(jnp.bfloat16)
    keyvals = jnp.dot(normed, keyval_weight, preferred_element_type=jnp.float32).astype(
        jnp.bfloat16
    )
    pooled = jnp.mean(
        widened.reshape(coarse_rows // PAIR_POOL, PAIR_POOL, model_dim), axis=1
    ).astype(jnp.bfloat16)
    pair_feats = jnp.dot(pooled, pair_weight, preferred_element_type=jnp.float32).astype(
        jnp.bfloat16
    )
    pair_q = pair_feats[:, :pair_dim]
    pair_k = pair_feats[:, pair_dim:]
    keys_all, pairk_all = (
        lax.all_gather(keyvals[None], ("seq", "mp"), axis=1, tiled=True),
        lax.all_gather(pair_k[None], ("seq", "mp"), axis=1, tiled=True),
    )
    summed = (
        pair_input[0].astype(jnp.float32)
        + pair_q[:, None, :].astype(jnp.float32) * pairk_all[0][None, :, :].astype(jnp.float32)
    ).astype(jnp.bfloat16)
    flipped = lax.all_to_all(summed[None], ("seq", "mp"), split_axis=2, concat_axis=1, tiled=True)[
        0
    ]
    turned = jnp.einsum("bac,cd->abd", flipped, flip_weight, preferred_element_type=jnp.float32)
    pair_out = (summed.astype(jnp.float32) + turned).astype(jnp.bfloat16)
    grad_term = jnp.einsum(
        "bac,abd->cd", flipped, pair_cotangent[0], preferred_element_type=jnp.float32
    )
    grad_flip = lax.psum(grad_term, ("dp", "seq", "mp"))
    key_rows = keys_all[0][:, :key_dim]
    value_rows = keys_all[0][:, key_dim:]
    query_rows = queries.reshape(coarse_rows * head_count, key_dim)
    scores = jnp.dot(query_rows, key_rows.T, preferred_element_type=jnp.float32)
    weights = jnp.exp(logit_cap * jnp.tanh(scores / logit_cap))
    totals = jnp.sum(weights, axis=-1, keepdims=True)
    mixed = (
        jnp.dot(weights.astype(jnp.bfloat16), value_rows, preferred_element_type=jnp.float32)
        / totals
    )
    heads_out = mixed.astype(jnp.bfloat16).reshape(coarse_rows, head_count * value_rows.shape[1])
    block_out = (
        widened + jnp.dot(heads_out, output_weight, preferred_element_type=jnp.float32)
    ).astype(jnp.bfloat16)
    return (block_out[None], pair_out[None], grad_flip)


def solution(mesh):
    placed = (
        P("dp", ("seq", "mp"), None),
        P(None, ("seq", "mp"), None),
        P(),
        P(),
        P(),
        P(),
        P(),
        P(),
        P("dp", ("seq", "mp"), None, None),
        P(),
        P("dp", ("seq", "mp"), None, None),
    )
    return jax.shard_map(
        per_device,
        mesh=mesh,
        in_specs=placed,
        out_specs=(P("dp", ("seq", "mp"), None), P("dp", ("seq", "mp"), None, None), P()),
        check_vma=False,
    )
```

profile of v0, /device:TPU:1, one launch (start us, length us, event | category | flops | bytes accessed | tf_op | source)
XLA Modules:
  0.0 959.2 jit_solution(9439417309653292819)
XLA Ops:
  7.2 2.7 copy.24
  10.0 0.8 fusion.84
  10.7 1.3 collective-permute-start.1
  12.0 10.3 %collective-permute-start = (bf16[1,2,1408]{2,1,0:T(2,128)(2,1)S(1)}, bf16[1,2,1408]{2,1,0:T(2,128)(2,1)S(1)}, u32[]{:S(2)}, u32[]{:S(2)}) collective-permute-start(bf16[1,2,1408]{2,1,0:T(2,128)(2,1)S(1)} %get-tuple-element.8), channel_id=1, source_target_pairs={{0,1},{1,2},{2,3},{3,4},{4,5},{5,6},{6,7},{7,8},{8,9},{9,10},{10,1... | collective-permute-start | bytes 16904 | tf_op jit(solution)/shard_map/ppermute | solution.py:22
  23.1 1.4 fusion.48
  24.5 6.0 fusion.20
  30.5 426.3 %all-gather.5.cloned.1.call-done = bf16[5,1408,1536]{2,0,1:T(8,128)(2,1)} async-done(((bf16[5,44,1536]{2,0,1:T(8,128)(2,1)}), bf16[5,1408,1536]{2,0,1:T(8,128)(2,1)}) %all-gather.5.cloned.1.call-update) | async-done | bytes 21626896 | tf_op jit(solution)/shard_map/all_gather | solution.py:76
  456.8 92.6 %fusion.83 = (bf16[1,1408,1536]{2,0,1:T(2,128)(2,1)S(1)}, bf16[1,1408,1536]{2,0,1:T(2,128)(2,1)S(1)}, bf16[1,1408,1536]{2,0,1:T(2,128)(2,1)}, bf16[1,1408,1536]{2,0,1:T(2,128)(2,1)}, bf16[1,1408,1536]{2,0,1:T(2,128)(2,1)}) fusion(bf16[5,1408,1536]{2,0,1:T(8,128)(2,1)} %all-gather.5.cloned.1.call-done), kind=kLoop, calls=%fused_computation.101 | loop fusion | bytes 43253760 | tf_op jit(solution)/shard_map/slice | solution.py:40
  549.4 5.0 fusion.7
  554.5 4.9 fusion.9
  559.4 1.4 fusion.10
  560.8 1.4 fusion.11
  562.3 2.3 fusion.13
  564.6 2.9 reshape.58
  567.5 3.0 reduce_max.9
  570.7 2.3 convolution_convert_fusion
  573.2 1.4 convolution_convert_fusion.1
  574.6 105.2 %all-gather.1 = bf16[256,128]{1,0:T(8,128)(2,1)S(1)} all-gather(bf16[8,128]{1,0:T(8,128)(2,1)S(1)} %get-tuple-element.11), channel_id=3, replica_groups=mesh['dp'=8,'seq'=16,'mp'=2] {'seq','mp'}, dimensions={0}, use_global_device_ids=true | all-gather | bytes 67584 | tf_op jit(solution)/shard_map/all_gather | solution.py:101
  680.5 1.1 copy.31
  681.6 4.6 all-to-all-start
  687.0 1.3 fusion.52
  688.3 1.8 reshape.59
  690.1 9.7 %all-to-all-done = bf16[1,8,256,128]{3,1,0,2:T(8,128)(2,1)} async-done(((bf16[1,8,256,128]{3,1,0,2:T(8,128)(2,1)}), bf16[1,8,256,128]{3,1,0,2:T(8,128)(2,1)}, u32[]{:S(2)}, u32[]{:S(2)}) %all-to-all-start) | async-done | bytes 524320 | tf_op jit(solution)/shard_map/all_to_all | solution.py:107
  699.8 2.2 convolution_bitcast_fusion.1
  702.0 2.3 fusion.51
  704.4 6.7 fusion
  711.1 5.9 fusion.63
  717.0 2.0 copy.30
  719.0 2.3 reshape.60
  721.3 4.0 fusion.15
  725.3 225.9 %all-reduce.3.cloned.1.call-done = f32[128,128]{1,0:T(8,128)} async-done(((f32[128,128]{1,0:T(8,128)}), f32[128,128]{1,0:T(8,128)}) %all-reduce.3.cloned.1.call-update) | async-done | bytes 65552 | tf_op jit(solution)/shard_map/psum | solution.py:115
  951.2 1.5 copy.69
  (39 shorter events, 2.7 us)
Async XLA Ops:
  7.2 679.8 %copy-start = (bf16[1536,1024]{1,0:T(8,128)(2,1)S(1)}, bf16[1536,1024]{1,0:T(8,128)(2,1)}, u32[]{:S(2)}) copy-start(bf16[1536,1024]{1,0:T(8,128)(2,1)} %param.14) | copy-start | bytes 9437188
  7.2 449.6 %all-gather.5.cloned.1.call-start = ((), (), s32[]{:S(2)}) async-start(), calls=%async_computation.1 | async-start | bytes 35684352 | tf_op jit(solution)/shard_map/all_gather | solution.py:76
  9.9 694.5 %all-gather.7.cloned.1.call-start = ((), (), s32[]{:S(2)}) async-start(), calls=%async_computation.3 | async-start | bytes 2703360 | tf_op jit(solution)/shard_map/all_gather | solution.py:100
  10.7 11.6 %collective-permute-start.1 = (bf16[1,2,1408]{2,1,0:T(2,128)(2,1)S(1)}, bf16[1,2,1408]{2,1,0:T(2,128)(2,1)S(1)}, u32[]{:S(2)}, u32[]{:S(2)}) collective-permute-start(bf16[1,2,1408]{2,1,0:T(2,128)(2,1)S(1)} %get-tuple-element.9), channel_id=1, source_target_pairs={{1,0},{2,1},{3,2},{4,3},{5,4},{6,5},{7,6},{8,7},{9,8},{10,9},{11,1... | collective-permute-start | bytes 16904 | tf_op jit(solution)/shard_map/ppermute | solution.py:23
  12.0 11.0 %collective-permute-start = (bf16[1,2,1408]{2,1,0:T(2,128)(2,1)S(1)}, bf16[1,2,1408]{2,1,0:T(2,128)(2,1)S(1)}, u32[]{:S(2)}, u32[]{:S(2)}) collective-permute-start(bf16[1,2,1408]{2,1,0:T(2,128)(2,1)S(1)} %get-tuple-element.8), channel_id=1, source_target_pairs={{0,1},{1,2},{2,3},{3,4},{4,5},{5,6},{6,7},{7,8},{8,9},{9,10},{10,1... | collective-permute-start | bytes 16904 | tf_op jit(solution)/shard_map/ppermute | solution.py:22
  456.8 92.6 %copy-start.4 = (bf16[260,1408]{1,0:T(8,128)(2,1)S(1)}, bf16[260,1408]{1,0:T(8,128)(2,1)}, u32[]{:S(2)}) copy-start(bf16[260,1408]{1,0:T(8,128)(2,1)} %fusion.20) | copy-start | bytes 2196484
  549.4 9.9 %slice-start = ((s8[8650752]{0:T(1024)(128)(4,1)}), s8[4194304]{0:T(1024)(128)(4,1)S(1)}, s32[]{:S(2)}) async-start(s8[8650752]{0:T(1024)(128)(4,1)} %bitcast.79), calls=%async_computation.4 | async-start | bytes 8388608
  549.4 9.9 %slice-start.1 = ((s8[8650752]{0:T(1024)(128)(4,1)}), s8[4194304]{0:T(1024)(128)(4,1)S(1)}, s32[]{:S(2)}) async-start(s8[8650752]{0:T(1024)(128)(4,1)} %bitcast.79), calls=%async_computation.5 | async-start | bytes 8388608
  554.4 4.9 slice-start.2
  560.8 1.4 copy-start.1
  564.6 6.1 copy-start.5
  573.0 106.8 %copy-start.2 = (bf16[1,8,256,128]{3,2,1,0:T(8,128)(2,1)S(1)}, bf16[1,8,256,128]{3,2,1,0:T(8,128)(2,1)}, u32[]{:S(2)}) copy-start(bf16[1,8,256,128]{3,2,1,0:T(8,128)(2,1)} %param.19) | copy-start | bytes 1572868
  679.8 0.6 copy-start.3
  681.6 18.2 %all-to-all-start = ((bf16[1,8,256,128]{3,1,0,2:T(8,128)(2,1)}), bf16[1,8,256,128]{3,1,0,2:T(8,128)(2,1)}, u32[]{:S(2)}, u32[]{:S(2)}) async-start(bf16[1,8,256,128]{3,1,0,2:T(8,128)(2,1)} %copy.31), calls=%async_computation | async-start | bytes 1048576 | tf_op jit(solution)/shard_map/all_to_all | solution.py:107
  686.2 264.9 %all-reduce.3.cloned.1.call-start = ((), (), s32[]{:S(2)}) async-start(), calls=%async_computation.2 | async-start | bytes 131072 | tf_op jit(solution)/shard_map/psum | solution.py:115
  704.4 6.7 copy-start.6
Sparse Core Ops, SparseCore 0:
  11.4 445.3 all-gather.4
  573.2 103.0 all-gather.6
  704.5 246.6 all-reduce.2
where the time goes:
time: 960 us; the launch traced here: 959 us
  waiting for transfers between devices  663 us (69%)
  local copies, waits for them, and re-layouts  108 us (11%)
  blocking collectives  105 us (11%)
  matrix products  41.2 us (4%)
  starting transfers between devices  16.3 us (2%)
  between operations  14 us (1%)
  other arithmetic  11.6 us (1%)
    all_gather x1, waiting for transfers between devices, per_device(): lax.all_gather(conv_weight, ('seq', 'mp'), axis=1, tiled=True)  426 us
    psum x1, waiting for transfers between devices, per_device(): grad_flip = lax.psum(grad_term, ('dp', 'seq', 'mp'))  226 us
    all_gather x1, blocking collectives, per_device(): lax.all_gather(pair_k[None], ('seq', 'mp'), axis=1, tiled=True)  105 us
    slice x1, local copies, waits for them, and re-layouts, tap_sum(): filter_rows[lag_index]  92.6 us
  transfers between devices with their start and end apart: 6, of which 4 were waited for; matrix products, arithmetic and copies ran while one was open for 4% of the time, Pallas kernels for 0%

commit v1 on v0

v1 whole, which is shorter than its diff:
```python
import functools
import math

import jax
import jax.numpy as jnp
import numpy as np
from jax import lax
from jax.experimental import pallas as pl
from jax.experimental.pallas import tpu as pltpu
from jax.sharding import PartitionSpec as P

MESH = pl.DeviceIdType.MESH
PAIR_POOL = 16
SIDE = 4
CORES = 2
Z_LO = 4
norm_eps = 1e-06
logit_cap = 50.0


def root_norm(values_in):
    return values_in * lax.rsqrt(jnp.mean(values_in * values_in, axis=-1, keepdims=True) + norm_eps)


def prepare(raw):
    return jax.nn.gelu(root_norm(raw.astype(jnp.float32)), approximate=False).astype(jnp.bfloat16)


def rcopy(src, dst, ssem, rsem, dev):
    return pltpu.make_async_remote_copy(
        src_ref=src, dst_ref=dst, send_sem=ssem, recv_sem=rsem, device_id=dev, device_id_type=MESH
    )


class Gather:
    def __init__(self, buf, own_src, rows, cut, zsend, zrecv, ssem, rsem, lsem, mirror=False):
        self.mirror = mirror
        self.buf, self.own_src, self.rows, self.cut = buf, own_src, rows, cut
        self.zsend, self.zrecv, self.ssem, self.rsem, self.lsem = zsend, zrecv, ssem, rsem, lsem
        self.dp, self.seq, self.mp = (lax.axis_index(a) for a in ("dp", "seq", "mp"))
        self.x, self.y = self.seq // SIDE, self.seq % SIDE
        self.count = 0
        self.sent = []
        self.pending_local = []

    def z_partner(self):
        if not self.mirror:
            return {"mp": 1 - self.mp}
        core, z = self.dp % CORES, self.dp // CORES
        return {"dp": (Z_LO - 1 - z) * CORES + core, "mp": 1 - self.mp}

    def peers(self):
        out = [self.z_partner()]
        for q in (0, 1):
            for d in (1, -1):
                out.append({"seq": self.bid(q, d, 0)})
        return out

    def bid(self, q, da, db):
        first, second = (self.x, self.y) if q == 0 else (self.y, self.x)
        a, b = (first + da + SIDE) % SIDE, (second + db + SIDE) % SIDE
        return a * SIDE + b if q == 0 else b * SIDE + a

    def z_of(self, zsel):
        return self.mp if zsel == 0 else 1 - self.mp

    def view(self, q, zsel, da, db, half):
        ref = self.buf.at[q, self.z_of(zsel), self.bid(q, da, db)]
        if half == 0:
            return ref.at[pl.ds(0, self.cut)]
        if half == 1:
            return ref.at[pl.ds(self.cut, self.rows - self.cut)]
        return ref

    def sem(self, q, zsel, da, db, half):
        return self.rsem.at[q, self.z_of(zsel), self.bid(q, da, db), 1 if half == 1 else 0]

    def send(self, q, zsel, da, db, half, to, src=None):
        view = self.view(q, zsel, da, db, half)
        copy = rcopy(view if src is None else src, view, self.ssem.at[self.count],
                     self.sem(q, zsel, da, db, half), {"seq": self.bid(q, *to)})
        self.count += 1
        copy.start()
        self.sent.append(copy)

    def recv(self, q, zsel, da, db, half=None):
        view = self.view(q, zsel, da, db, half)
        rcopy(view, view, self.ssem.at[0], self.sem(q, zsel, da, db, half), {"seq": self.bid(q, 1, 0)}).wait_recv()

    def start_z(self):
        for q in (0, 1):
            copy = rcopy(self.own_src(q), self.view(q, 0, 0, 0, None), self.zsend.at[q], self.zrecv.at[q], self.z_partner())
            copy.start()
            self.sent.append(copy)
            local = pltpu.make_async_copy(self.own_src(q), self.view(q, 0, 0, 0, None), self.lsem.at[q])
            local.start()
            self.pending_local.append(local)

    def stage(self, q, zsel, n):
        if n == 0:
            src = self.own_src(q) if zsel == 0 else None
            if zsel == 1:
                view = self.view(q, 1, 0, 0, None)
                rcopy(view, view, self.zsend.at[q], self.zrecv.at[q], self.z_partner()).wait_recv()
            for to in ((1, 0), (-1, 0), (0, 1), (0, -1)):
                self.send(q, zsel, 0, 0, None, to, src)
        elif n in (1, 2):
            d = -1 if n == 1 else 1
            self.recv(q, zsel, d, 0)
            self.send(q, zsel, d, 0, 0 if n == 1 else 1, (-d, 0))
            for to in ((0, 1), (0, -1)):
                self.send(q, zsel, d, 0, None, to)
        elif n == 4:
            self.recv(q, zsel, 2, 0, 0)
            self.recv(q, zsel, 2, 0, 1)
            for to in ((0, 1), (0, -1)):
                self.send(q, zsel, 2, 0, None, to)
        elif n in (3, 5, 6, 7):
            da = {3: 0, 5: -1, 6: 1, 7: 2}[n]
            for d, half in ((-1, 0), (1, 1)):
                self.recv(q, zsel, da, d)
                self.send(q, zsel, da, d, half, (0, -d))
        else:
            for da in (0, -1, 1, 2):
                for half in (0, 1):
                    self.recv(q, zsel, da, 2, half)

    def drain(self):
        for copy in self.sent:
            copy.wait_send()


ORDER = [(0, 0), (0, 1), (0, 2), (0, 3), (1, 0), (0, 4), (0, 5), (0, 6), (1, 1), (1, 2), (0, 7), (1, 3), (1, 4), (1, 5), (1, 6), (1, 7)]
GATHER_SENDS = 80


def gather_sems():
    dma = pltpu.SemaphoreType.DMA
    return [dma((2,)), dma((2,)), dma((GATHER_SENDS,)), dma((2, 2, SIDE * SIDE, 2)), dma((2,))]


def greet(peers):
    barrier = pltpu.get_barrier_semaphore()
    for peer in peers:
        pl.semaphore_signal(barrier, inc=1, device_id=peer, device_id_type=MESH)
    pl.semaphore_wait(barrier, len(peers))


def conv_kernel(
    w_ref, prep_ref, edge_ref, skip_ref, chan_ref, enc_ref,
    F, X, P2, S2, H, acc, stage, zs, zr, ss, rs, ls, xs, xr,
):
    dp, seq, mp = (lax.axis_index(a) for a in ("dp", "seq", "mp"))
    core = dp % CORES
    other = dp - core + (1 - core)
    rows, cut = w_ref.shape[1], 112
    taps, depth = 5, rows // 5
    width = w_ref.shape[2]
    g = Gather(F, lambda q: w_ref.at[CORES * core + q], rows, cut, zs, zr, ss, rs, ls, mirror=True)
    place = seq * 2 + mp
    last_place = SIDE * SIDE * 2 - 1
    after, before = (place + 1) % (last_place + 1), (place + last_place) % (last_place + 1)

    def at(p, d):
        return {"dp": d, "seq": p // 2, "mp": p % 2}

    partner = {"dp": other}
    greet(g.peers() + [partner, at(after, dp), at(after, other), at(before, dp), at(before, other)])

    g.start_z()
    extra = []
    n = 0
    for w, d in ((0, dp), (1, other)):
        extra.append(rcopy(edge_ref.at[1], H.at[w, 0], xs.at[n], xr.at[n], at(after, d)))
        extra.append(rcopy(edge_ref.at[0], H.at[w, 1], xs.at[n + 1], xr.at[n + 1], at(before, d)))
        n += 2
    extra.append(rcopy(prep_ref, P2, xs.at[4], xr.at[4], partner))
    extra.append(rcopy(skip_ref.at[pl.ds(CORES * (1 - core), 2)], S2, xs.at[5], xr.at[5], partner))
    for copy in extra:
        copy.start()
    for q in (0, 1):
        g.stage(q, 0, 0)

    def spread(w, n):
        zabs, lanes = n // 3, pl.ds((n % 3) * 256, 256)
        chan = chan_ref[:, n * 256 : (n + 1) * 256]
        cin = prep_ref.shape[2]
        pick = (lax.broadcasted_iota(jnp.int32, (cin, 256), 0) == chan).astype(jnp.float32).astype(jnp.bfloat16)
        src = prep_ref if w == 0 else P2
        height = src.shape[1]
        dot = functools.partial(jnp.dot, preferred_element_type=jnp.float32)
        even, odd = dot(src[0], pick), dot(src[1], pick)
        prev, nxt = dot(H[w, 0], pick), dot(H[w, 1], pick)
        prev = jnp.where(place == 0, 0.0, prev)
        nxt = jnp.where(place == last_place, 0.0, nxt)
        row = lax.broadcasted_iota(jnp.int32, (height, 256), 0)
        for m, (arr, halo, shift) in enumerate((
            (even, prev[14:15], 1), (odd, prev[15:16], 1), (even, None, 0), (odd, None, 0),
            (even, nxt[0:1], -1), (odd, nxt[1:2], -1),
        )):
            if shift == 1:
                arr = jnp.where(row == 0, halo, pltpu.roll(arr, 1, 0))
            elif shift == -1:
                arr = jnp.where(row == height - 1, halo, pltpu.roll(arr, height - 1, 0))
            X[w, zabs, m, :, lanes] = arr.astype(jnp.bfloat16)

    def do_spread(k):
        w, n = divmod(k, 6)
        if k == 0:
            for copy in extra:
                copy.wait_recv()
        spread(w, n)

    todo = list(range(12))
    for i, (zsel, st) in enumerate(ORDER[1:]):
        if i >= 1 and todo:
            do_spread(todo.pop(0))
        for q in (0, 1):
            g.stage(q, zsel, st)
    while todo:
        do_spread(todo.pop(0))

    for local in g.pending_local:
        local.wait()

    def conv(zsel):
        za = g.z_of(zsel)
        for q in (0, 1):
            def tap(k, carry):
                lhs = X[:, za, pl.ds(k, 2)].reshape(acc.shape[1], -1)
                rhs = F[q, za, :, pl.ds(pl.multiple_of(k * depth, 16), depth), :].reshape(-1, width)
                acc[q] += jnp.dot(lhs, rhs, preferred_element_type=jnp.float32)
                return carry
            lax.fori_loop(0, taps, tap, 0)

    acc[...] = jnp.zeros_like(acc)
    for q in (0, 1):
        g.stage(q, 0, 8)
    conv(0)
    for q in (0, 1):
        g.stage(q, 1, 8)
    conv(1)
    half = acc.shape[1] // 2
    coarse = half // 2
    finals = []
    for q in (0, 1):
        total = acc[q, half:] + S2[q].astype(jnp.float32)
        stage[q] = jnp.maximum(total[:coarse], total[coarse:]).astype(jnp.bfloat16)
        copy = rcopy(stage.at[q], enc_ref.at[CORES * core + q], xs.at[6 + q], xr.at[6 + q], partner)
        copy.start()
        finals.append(copy)
    for q in (0, 1):
        total = acc[q, :half] + skip_ref[CORES * core + q].astype(jnp.float32)
        enc_ref[CORES * core + q] = jnp.maximum(total[:coarse], total[coarse:]).astype(jnp.bfloat16)
    for q in (0, 1):
        view = enc_ref.at[CORES * (1 - core) + q]
        rcopy(stage.at[q], view, xs.at[6 + q], xr.at[6 + q], partner).wait_recv()
    g.drain()
    for copy in extra + finals:
        copy.wait_send()


def encode(w4, prep, edge, skip, chan):
    vm = pl.BlockSpec(memory_space=pltpu.VMEM)
    dma = pltpu.SemaphoreType.DMA
    quarters, rows, width = w4.shape
    coarse = prep.shape[1]
    kdepth = SIDE * SIDE * rows // 5
    return pl.pallas_call(
        conv_kernel,
        out_shape=jax.ShapeDtypeStruct((quarters, coarse, width), jnp.bfloat16),
        in_specs=[vm] * 5,
        out_specs=vm,
        scratch_shapes=[
            pltpu.VMEM((2, 2, SIDE * SIDE, rows, width), jnp.bfloat16),
            pltpu.VMEM((2, 2, 6, coarse, kdepth), jnp.bfloat16),
            pltpu.VMEM(prep.shape, jnp.bfloat16),
            pltpu.VMEM((2, 2 * coarse, width), jnp.bfloat16),
            pltpu.VMEM((2, 2, 16, prep.shape[2]), jnp.bfloat16),
            pltpu.VMEM((2, 4 * coarse, width), jnp.float32),
            pltpu.VMEM((2, coarse, width), jnp.bfloat16),
        ] + gather_sems() + [dma((8,)), dma((8,))],
        compiler_params=pltpu.CompilerParams(collective_id=0, has_side_effects=True, vmem_limit_bytes=60 << 20),
        name="encode",
    )(w4, prep, edge, skip, chan)


def share_kernel(src_ref, out_ref, zs, zr, ss, rs, ls):
    rows = src_ref.shape[1]
    g = Gather(out_ref, lambda q: src_ref.at[q], rows, rows // 2, zs, zr, ss, rs, ls)
    greet(g.peers())
    g.start_z()
    for zsel, st in ORDER + [(0, 8), (1, 8)]:
        for q in (0, 1):
            g.stage(q, zsel, st)
    for local in g.pending_local:
        local.wait()
    g.drain()


def share(src):
    vm = pl.BlockSpec(memory_space=pltpu.VMEM)
    return pl.pallas_call(
        share_kernel,
        out_shape=jax.ShapeDtypeStruct((2, 2, SIDE * SIDE) + src.shape[1:], src.dtype),
        in_specs=[vm],
        out_specs=vm,
        scratch_shapes=gather_sems(),
        compiler_params=pltpu.CompilerParams(collective_id=1, has_side_effects=True, vmem_limit_bytes=32 << 20),
        name="share",
    )(src)


def total_kernel(g_ref, out_ref, R1, R2, fin, s1, r1, s2, r2, s3, r3):
    dp, seq, mp = (lax.axis_index(a) for a in ("dp", "seq", "mp"))
    n1, n2 = SIDE * SIDE, Z_LO * CORES * 2
    rows = g_ref.shape[0] // n1
    plane = [{"seq": (seq + d) % n1} for d in range(1, n1)]
    mine = dp * 2 + mp
    column = []
    for d in range(1, n2):
        t = (mine + d) % n2
        column.append({"dp": t // 2, "mp": t % 2})
    greet(plane + column)
    sent = []
    for d, dev in enumerate(plane):
        c = rcopy(g_ref.at[pl.ds(pl.multiple_of(dev["seq"] * rows, rows), rows)], R1.at[seq], s1.at[d], r1.at[seq], dev)
        c.start()
        sent.append(c)
    own = g_ref[pl.ds(pl.multiple_of(seq * rows, rows), rows)]
    R1[seq] = own
    for d, dev in enumerate(plane):
        view = R1.at[dev["seq"]]
        rcopy(view, view, s1.at[d], r1.at[dev["seq"]], dev).wait_recv()
    fin[0] = jnp.sum(R1[...], axis=0)
    for d, dev in enumerate(column):
        c = rcopy(fin.at[0], R2.at[mine], s2.at[d], r2.at[mine], dev)
        c.start()
        sent.append(c)
    R2[mine] = fin[0]
    for d, dev in enumerate(column):
        t = dev["dp"] * 2 + dev["mp"]
        rcopy(R2.at[t], R2.at[t], s2.at[d], r2.at[t], dev).wait_recv()
    fin[1] = jnp.sum(R2[...], axis=0)
    piece = pl.ds(pl.multiple_of(seq * rows, rows), rows)
    for d, dev in enumerate(plane):
        c = rcopy(fin.at[1], out_ref.at[piece], s3.at[d], r3.at[seq], dev)
        c.start()
        sent.append(c)
    out_ref[piece] = fin[1]
    for d, dev in enumerate(plane):
        view = out_ref.at[pl.ds(pl.multiple_of(dev["seq"] * rows, rows), rows)]
        rcopy(view, view, s3.at[d], r3.at[dev["seq"]], dev).wait_recv()
    for c in sent:
        c.wait_send()


def total(term):
    vm = pl.BlockSpec(memory_space=pltpu.VMEM)
    dma = pltpu.SemaphoreType.DMA
    rows = term.shape[0] // (SIDE * SIDE)
    n = SIDE * SIDE
    block = (n, rows, term.shape[1])
    return pl.pallas_call(
        total_kernel,
        out_shape=jax.ShapeDtypeStruct(term.shape, term.dtype),
        in_specs=[vm],
        out_specs=vm,
        scratch_shapes=[pltpu.VMEM(block, jnp.float32), pltpu.VMEM(block, jnp.float32), pltpu.VMEM((2,) + block[1:], jnp.float32)]
        + [dma((n,))] * 6,
        compiler_params=pltpu.CompilerParams(collective_id=2, has_side_effects=True, vmem_limit_bytes=16 << 20),
        name="total",
    )(term)


def per_device(
    features, conv_weight, norm_gain, query_weight, keyval_weight, head_scale, output_weight, pair_weight,
    pair_input, flip_weight, pair_cotangent,
):
    fine_rows, in_channels = features.shape[1:]
    coarse = fine_rows // 2
    model_dim = output_weight.shape[1]
    head_count = head_scale.shape[0]
    key_dim = query_weight.shape[1] // head_count
    value_dim = keyval_weight.shape[1] - key_dim
    pair_dim = flip_weight.shape[0]
    taps, per_shard = conv_weight.shape[:2]
    padded = 48
    quarter = model_dim // 4

    w4 = jnp.pad(conv_weight, ((0, 0), (0, padded - per_shard), (0, 0)))
    w4 = w4.reshape(taps * padded, 4, quarter).transpose(1, 0, 2)
    prepared = prepare(features[0])
    edge = jnp.stack([prepared[:16], prepared[fine_rows - 16 :]])
    prep = prepared.reshape(coarse, 2, in_channels).transpose(1, 0, 2)
    skip = jnp.pad(features[0], ((0, 0), (0, model_dim - in_channels)))
    skip = skip.reshape(coarse, 2, 4, quarter).transpose(2, 1, 0, 3).reshape(4, fine_rows, quarter)
    lane = np.arange(2 * SIDE * SIDE * padded)
    zh, sq, ch = lane // (SIDE * SIDE * padded), (lane // padded) % (SIDE * SIDE), lane % padded
    chan = np.where(ch < per_shard, per_shard * (2 * sq + zh) + ch, -1).astype(np.int32)[None]
    enc4 = encode(w4, prep, edge, skip, jnp.asarray(chan))
    encoded = enc4.transpose(1, 0, 2).reshape(coarse, model_dim)

    turned_in = lax.all_to_all(pair_input, ("seq", "mp"), split_axis=2, concat_axis=1, tiled=True)[0]

    widened = encoded.astype(jnp.float32)
    normed = (root_norm(widened) * norm_gain).astype(jnp.bfloat16)
    keyvals = jnp.dot(normed, keyval_weight, preferred_element_type=jnp.float32).astype(jnp.bfloat16)
    pooled = jnp.mean(widened.reshape(coarse // PAIR_POOL, PAIR_POOL, model_dim), axis=1).astype(jnp.bfloat16)
    feats = jnp.dot(pooled, pair_weight, preferred_element_type=jnp.float32).astype(jnp.bfloat16)
    pair_rows = feats.shape[0]
    spare = jnp.pad(feats.reshape(-1, 64), ((0, coarse - feats.size // 64), (0, 0)))
    block = jnp.concatenate([keyvals, spare], axis=1).reshape(2, coarse // 2, -1)
    shared = share(block)
    scale_row = jnp.repeat(head_scale, key_dim) / math.sqrt(key_dim)
    queries = (jnp.dot(normed, query_weight, preferred_element_type=jnp.float32) * scale_row).astype(jnp.bfloat16)

    feats_all = shared[0, :, :, : feats.size // 64, key_dim + value_dim :]
    feats_all = feats_all.transpose(1, 0, 2, 3).reshape(-1, 2 * pair_dim).astype(jnp.float32)
    pair_q, pair_k = feats[:, :pair_dim].astype(jnp.float32), feats[:, pair_dim:].astype(jnp.float32)
    q_all, k_all = feats_all[:, :pair_dim], feats_all[:, pair_dim:]
    summed = (pair_input[0].astype(jnp.float32) + pair_q[:, None, :] * k_all[None]).astype(jnp.bfloat16)
    flipped = (turned_in.astype(jnp.float32) + q_all[:, None, :] * pair_k[None]).astype(jnp.bfloat16)
    turned = jnp.einsum("bac,cd->abd", flipped, flip_weight, preferred_element_type=jnp.float32)
    pair_out = (summed.astype(jnp.float32) + turned).astype(jnp.bfloat16)
    grad_term = jnp.einsum("bac,abd->cd", flipped, pair_cotangent[0], preferred_element_type=jnp.float32)
    grad_flip = total(grad_term)

    flat = shared.reshape(-1, shared.shape[-1])
    key_rows, value_rows = flat[:, :key_dim], flat[:, key_dim : key_dim + value_dim]
    query_rows = queries.reshape(coarse * head_count, key_dim)
    scores = jnp.dot(query_rows, key_rows.T, preferred_element_type=jnp.float32)
    weights = jnp.exp(logit_cap * jnp.tanh(scores / logit_cap))
    totals = jnp.sum(weights, axis=-1, keepdims=True)
    mixed = jnp.dot(weights.astype(jnp.bfloat16), value_rows, preferred_element_type=jnp.float32) / totals
    heads_out = mixed.astype(jnp.bfloat16).reshape(coarse, head_count * value_dim)
    block_out = (widened + jnp.dot(heads_out, output_weight, preferred_element_type=jnp.float32)).astype(jnp.bfloat16)
    return (block_out[None], pair_out[None], grad_flip)


def solution(mesh):
    rows = P("dp", ("seq", "mp"), None)
    pair = P("dp", ("seq", "mp"), None, None)
    placed = (rows, P(None, ("seq", "mp"), None), P(), P(), P(), P(), P(), P(), pair, P(), pair)
    return jax.shard_map(per_device, mesh=mesh, in_specs=placed, out_specs=(rows, pair, P()), check_vma=False)
```

time: 960 us -> 242 us (0.25)
  waiting for transfers between devices: 663 us -> 0.01 us
  Pallas kernels: 0 us -> 140 us
  blocking collectives: 105 us -> 0 us
  local copies, waits for them, and re-layouts: 108 us -> 39.5 us
  matrix products: 41.2 us -> 27.7 us
  between operations: 14 us -> 0.88 us
    all_gather x2 -> x0, waiting for transfers between devices: 426 us -> none  [the longest x1 426 us: per_device(): lax.all_gather(conv_weight, ('seq', 'mp'), axis=1, tiled=True)]
    psum x1 -> x0, waiting for transfers between devices: 226 us -> none  [per_device(): grad_flip = lax.psum(grad_term, ('dp', 'seq', 'mp'))]
    pallas_call x0 -> x3, Pallas kernels: none -> 140 us  [the longest x1 88.2 us: encode(): pl.pallas_call(conv_kernel, out_shape=jax.ShapeDtypeStruct((quarters, coa...]
    all_gather x1 -> x0, blocking collectives: 105 us -> none  [per_device(): lax.all_gather(pair_k[None], ('seq', 'mp'), axis=1, tiled=True)]
    slice x2 -> x1, local copies, waits for them, and re-layouts: 93.4 us -> 1.68 us  [per_device(): q_all, k_all = (feats_all[:, :pair_dim], feats_all[:, pair_dim:])]
    dot_general x5 -> x0, matrix products: 15.1 us -> none  [tap_sum(): jnp.dot(source[lag_index:lag_index + out_rows], filter_rows[lag_index], p...]
    convert_element_type x2 -> x9, local copies, waits for them, and re-layouts: 3.14 us -> 16.3 us  [the longest x4 9.47 us: per_device(): widened = encoded.astype(jnp.float32)]
    ppermute x2 -> x0, starting transfers between devices: 11.6 us -> none  [the longest x1 10.3 us: padded_2(): before = lax.ppermute(last, axis, up)]
  transfers between devices with their start and end apart: 6 -> 1, of which waited for: 4 -> 0; matrix products, arithmetic and copies ran while one was open for 4% -> 32% of each run, Pallas kernels for 0% -> 49%
where the time goes in v1:
time: 242 us; the launch traced here: 241 us
  Pallas kernels  140 us (58%)
  local copies, waits for them, and re-layouts  39.5 us (16%)
  matrix products  27.7 us (11%)
  other arithmetic  18.4 us (8%)
  starting transfers between devices  14.6 us (6%)
    pallas_call x1, Pallas kernels, encode(): pl.pallas_call(conv_kernel, out_shape=jax.ShapeDtypeStruct((quarters, coa...  88.2 us
    pallas_call x1, Pallas kernels, share(): pl.pallas_call(share_kernel, out_shape=jax.ShapeDtypeStruct((2, 2, SIDE *...  30.8 us
    pallas_call x1, Pallas kernels, total(): pl.pallas_call(total_kernel, out_shape=jax.ShapeDtypeStruct(term.shape, t...  20.6 us
    all_to_all x1, starting transfers between devices, per_device(): lax.all_to_all(pair_input, ('seq', 'mp'), split_axis=2, concat_axis=1, ti...  14.6 us
    convert_element_type x4, local copies, waits for them, and re-layouts, per_device(): widened = encoded.astype(jnp.float32)  9.47 us
    dot_general x1, matrix products, per_device(): scores = jnp.dot(query_rows, key_rows.T, preferred_element_type=jnp.float32)  9.36 us
    dot_general x1, matrix products, per_device(): jnp.dot(weights.astype(jnp.bfloat16), value_rows, preferred_element_type=...  9 us
    unnamed x32, local copies, waits for them, and re-layouts  5.5 us
  transfers between devices with their start and end apart: 1, of which 0 were waited for; matrix products, arithmetic and copies ran while one was open for 32% of the time, Pallas kernels for 49%

profile of v1, /device:TPU:1, one launch (start us, length us, event | category | flops | bytes accessed | tf_op | source)
XLA Modules:
  0.0 240.7 jit_solution(12368468819103109640)
XLA Ops:
  0.6 2.3 copy.58
  3.0 14.6 %all-to-all-start = ((bf16[1,8,256,128]{3,1,0,2:T(8,128)(2,1)}), bf16[1,8,256,128]{3,1,0,2:T(8,128)(2,1)}, u32[]{:S(2)}, u32[]{:S(2)}) async-start(bf16[1,8,256,128]{3,1,0,2:T(8,128)(2,1)} %copy.58), calls=%async_computation | async-start | bytes 1048576 | tf_op jit(solution)/shard_map/all_to_all | solution.py:404
  17.6 1.3 fusion.38
  19.0 5.1 %fusion.10 = bf16[256,1408]{1,0:T(8,128)(2,1)} fusion(f32[256]{0:T(256)S(1)} %add_rsqrt_fusion, bf16[1,256,1408]{2,1,0:T(8,128)(2,1)} %param.12), kind=kLoop, calls=%fused_computation.15 | loop fusion | flops 24150016 | bytes 1442816 | tf_op jit(solution)/shard_map/convert_element_type | solution.py:26
  24.2 2.9 %reshape.102 = f32[128,2,1408]{2,1,0:T(2,128)} reshape(bf16[1,256,1408]{2,1,0:T(8,128)(2,1)} %param.12) | data formatting | bytes 2162688 | tf_op jit(solution)/shard_map/convert_element_type | solution.py:26
  28.0 2.1 pad.13
  30.1 2.5 %reshape.95 = bf16[128,2,4,384]{3,2,1,0:T(4,128)(2,1)} reshape(bf16[256,1536]{1,0:T(8,128)(2,1)} %pad.13) | data formatting | bytes 1572864 | tf_op jit(solution)/shard_map/reshape | solution.py:397
  32.6 2.2 copy.50
  35.7 2.4 reshape.94
  38.1 2.2 copy.74
  41.0 4.1 %fusion.68.prep_ref = bf16[2,128,1408]{2,1,0:T(8,128)(2,1)} fusion(f32[128,2]{0,1:T(2,128)S(1)} %copy.48, f32[128,2,1408]{2,1,0:T(2,128)S(1)} %copy-done.3), kind=kLoop, calls=%fused_computation.86 | loop fusion | flops 23789568 | bytes 2163712 | tf_op jit(solution)/shard_map/transpose | solution.py:395
  45.1 88.2 %encode.1 = bf16[4,128,384]{2,1,0:T(8,128)(2,1)} custom-call(bf16[4,240,384]{2,1,0:T(8,128)(2,1)} %bitcast.75, bf16[2,128,1408]{2,1,0:T(8,128)(2,1)} %fusion.68.prep_ref, bf16[2,16,1408]{2,1,0:T(8,128)(2,1)} %pad_maximum_fusion.edge_ref, bf16[4,256,384]{2,1,0:T(8,128)(2,1)} %bitcast.74, s32[1,1536]{1,0:T(1,128)} %constant.85.clone.chan_ref), custom_call_target="tpu_custom_call" | custom-call | tf_op jit(solution)/shard_map/encode/pallas_call | solution.py:269
  133.3 2.0 convert_bitcast_fusion.1
  135.5 2.3 copy.51
  137.8 2.5 %copy.52 = f32[128,4,384]{2,1,0:T(4,128)} copy(f32[128,4,384]{2,0,1:T(8,128)} %convert_bitcast_fusion.1) | data formatting | bytes 1572864 | tf_op jit(solution)/shard_map/convert_element_type | solution.py:406
  140.3 2.3 reshape.104
  142.7 1.3 reduce_sum.38
  143.9 1.3 convolution_convert_fusion.1
  145.5 1.4 multiply_convert_fusion
  146.9 1.8 convolution_convert_fusion
  148.9 30.8 %share.1 = bf16[2,2,16,64,384]{4,3,2,1,0:T(8,128)(2,1)S(1)} custom-call(bf16[2,64,384]{2,1,0:T(8,128)(2,1)S(1)} %bitcast.71), custom_call_target="tpu_custom_call" | custom-call | tf_op jit(solution)/shard_map/share/pallas_call | solution.py:303
  179.7 1.6 copy-done.1
  182.8 9.4 %fusion = (f32[1024]{0:T(1024)S(1)}, f32[1024,4096]{1,0:T(8,128)}) fusion(bf16[1024,128]{1,0:T(8,128)(2,1)} %reshape.97, bf16[4096,384]{1,0:T(8,128)(2,1)} %bitcast.69), kind=kOutput, calls=%fused_computation.1 | convolution fusion | flops 1086323712 | bytes 18092032 | tf_op jit(solution)/shard_map/dot_general | solution.py:432
  192.2 9.0 %fusion.62 = bf16[1024,192]{0,1:T(8,128)(2,1)S(1)} fusion(bf16[4096,384]{1,0:T(8,128)(2,1)S(1)} %bitcast.70, f32[1024,4096]{1,0:T(8,128)} %get-tuple-element.10, f32[1024]{0:T(1024)S(1)} %get-tuple-element.9), kind=kOutput, calls=%fused_computation.82 | convolution fusion | flops 1623588864 | bytes 19271680 | tf_op jit(solution)/shard_map/dot_general | solution.py:435
  202.2 1.5 reshape.101
  203.7 2.3 copy.56
  208.0 1.9 reshape.106
  209.9 1.7 fusion.78
  211.6 4.1 %fusion.5 = bf16[1,128,1536]{2,1,0:T(8,128)(2,1)} fusion(f32[128,1536]{1,0:T(8,128)} %copy.56, bf16[128,1536]{1,0:T(8,128)(2,1)S(1)} %reshape.101, bf16[1536,1536]{1,0:T(8,128)(2,1)} %param.18), kind=kOutput, calls=%fused_computation.6 | convolution fusion | flops 604372992 | bytes 6291456 | tf_op jit(solution)/shard_map/dot_general | solution.py:437
  215.6 1.1 convert_bitcast_fusion
  218.4 20.6 %total.1 = f32[128,128]{1,0:T(8,128)S(1)} custom-call(f32[128,128]{1,0:T(8,128)S(1)} %convolution_bitcast_fusion.1.g_ref), custom_call_target="tpu_custom_call" | custom-call | tf_op jit(solution)/shard_map/total/pallas_call | solution.py:364
  239.0 1.1 fusion.51
  (54 shorter events, 9.8 us)
Async XLA Ops:
  0.6 180.8 %copy-start = (bf16[1536,1024]{1,0:T(8,128)(2,1)S(1)}, bf16[1536,1024]{1,0:T(8,128)(2,1)}, u32[]{:S(2)}) copy-start(bf16[1536,1024]{1,0:T(8,128)(2,1)} %param.15) | copy-start | bytes 9437188
  3.0 212.7 %all-to-all-start = ((bf16[1,8,256,128]{3,1,0,2:T(8,128)(2,1)}), bf16[1,8,256,128]{3,1,0,2:T(8,128)(2,1)}, u32[]{:S(2)}, u32[]{:S(2)}) async-start(bf16[1,8,256,128]{3,1,0,2:T(8,128)(2,1)} %copy.58), calls=%async_computation | async-start | bytes 1048576 | tf_op jit(solution)/shard_map/all_to_all | solution.py:404
  32.6 2.2 copy-start.8
  38.1 2.9 %copy-start.3 = (f32[128,2,1408]{2,1,0:T(2,128)S(1)}, f32[128,2,1408]{2,1,0:T(2,128)}, u32[]{:S(2)}) copy-start(f32[128,2,1408]{2,1,0:T(2,128)} %reshape.102) | copy-start | bytes 4325380
  133.3 2.0 copy-start.6
  140.3 5.2 %copy-start.12 = (f32[1536]{0:T(1024)S(1)}, f32[1536]{0:T(1024)}, u32[]{:S(2)}) copy-start(f32[1536]{0:T(1024)} %param.14) | copy-start | bytes 18436
  146.9 1.8 copy-start.4
  148.8 32.5 %copy-start.14 = (f32[8]{0:T(128)S(1)}, f32[8]{0:T(128)}, u32[]{:S(2)}) copy-start(f32[8]{0:T(128)} %param.17) | copy-start | bytes 100
  148.8 32.6 %copy-start.5 = (bf16[128,1536]{0,1:T(8,128)(2,1)S(1)}, bf16[128,1536]{0,1:T(8,128)(2,1)}, u32[]{:S(2)}) copy-start(bf16[128,1536]{0,1:T(8,128)(2,1)} %copy-done.4) | copy-start | bytes 1179652
  179.7 1.6 copy-start.1
  182.8 9.4 %copy-start.2 = (bf16[2,2,16,64,384]{4,3,2,1,0:T(8,128)(2,1)S(1)}, bf16[2,2,16,64,384]{4,3,2,1,0:T(8,128)(2,1)}, u32[]{:S(2)}) copy-start(bf16[2,2,16,64,384]{4,3,2,1,0:T(8,128)(2,1)} %copy-done.1) | copy-start | bytes 9437188
  216.8 0.9 copy-start.10
  216.8 1.1 copy-start.13
  217.9 21.1 %copy-start.7 = (bf16[1,8,256,128]{3,2,1,0:T(8,128)(2,1)S(1)}, bf16[1,8,256,128]{3,2,1,0:T(8,128)(2,1)}, u32[]{:S(2)}) copy-start(bf16[1,8,256,128]{3,2,1,0:T(8,128)(2,1)} %param.20) | copy-start | bytes 1572868
  217.9 21.1 %copy-start.9 = (f32[256,128]{1,0:T(8,128)S(1)}, f32[256,128]{1,0:T(8,128)}, u32[]{:S(2)}) copy-start(f32[256,128]{1,0:T(8,128)} %get-tuple-element.5) | copy-start | bytes 393220
  217.9 21.1 %copy-start.11 = (bf16[128,128]{1,0:T(8,128)(2,1)S(1)}, bf16[128,128]{1,0:T(8,128)(2,1)}, u32[]{:S(2)}) copy-start(bf16[128,128]{1,0:T(8,128)(2,1)} %param.21) | copy-start | bytes 98308

commit v2 on v1

--- a/solution.py
+++ b/solution.py
@@ -153,10 +153,14 @@
     dp, seq, mp = (lax.axis_index(a) for a in ("dp", "seq", "mp"))
     core = dp % CORES
     other = dp - core + (1 - core)
-    rows, cut = w_ref.shape[1], 112
+    rows, cut = w_ref.shape[0], 112
     taps, depth = 5, rows // 5
-    width = w_ref.shape[2]
-    g = Gather(F, lambda q: w_ref.at[CORES * core + q], rows, cut, zs, zr, ss, rs, ls, mirror=True)
+    width = F.shape[4]
+
+    def cols(n, count=1):
+        return pl.ds(pl.multiple_of(n * width, width), count * width)
+
+    g = Gather(F, lambda q: w_ref.at[:, cols(CORES * core + q)], rows, cut, zs, zr, ss, rs, ls, mirror=True)
     place = seq * 2 + mp
     last_place = SIDE * SIDE * 2 - 1
     after, before = (place + 1) % (last_place + 1), (place + last_place) % (last_place + 1)
@@ -175,7 +179,7 @@
         extra.append(rcopy(edge_ref.at[0], H.at[w, 1], xs.at[n + 1], xr.at[n + 1], at(before, d)))
         n += 2
     extra.append(rcopy(prep_ref, P2, xs.at[4], xr.at[4], partner))
-    extra.append(rcopy(skip_ref.at[pl.ds(CORES * (1 - core), 2)], S2, xs.at[5], xr.at[5], partner))
+    extra.append(rcopy(skip_ref.at[:, cols(CORES * (1 - core), 2)], S2, xs.at[5], xr.at[5], partner))
     for copy in extra:
         copy.start()
     for q in (0, 1):
@@ -244,71 +248,91 @@
     coarse = half // 2
     finals = []
     for q in (0, 1):
-        total = acc[q, half:] + S2[q].astype(jnp.float32)
+        total = acc[q, half:] + S2[:, q * width : (q + 1) * width].astype(jnp.float32)
         stage[q] = jnp.maximum(total[:coarse], total[coarse:]).astype(jnp.bfloat16)
-        copy = rcopy(stage.at[q], enc_ref.at[CORES * core + q], xs.at[6 + q], xr.at[6 + q], partner)
+        copy = rcopy(stage.at[q], enc_ref.at[:, cols(CORES * core + q)], xs.at[6 + q], xr.at[6 + q], partner)
         copy.start()
         finals.append(copy)
     for q in (0, 1):
-        total = acc[q, :half] + skip_ref[CORES * core + q].astype(jnp.float32)
-        enc_ref[CORES * core + q] = jnp.maximum(total[:coarse], total[coarse:]).astype(jnp.bfloat16)
-    for q in (0, 1):
-        view = enc_ref.at[CORES * (1 - core) + q]
+        total = acc[q, :half] + skip_ref[:, cols(CORES * core + q)].astype(jnp.float32)
+        enc_ref[:, cols(CORES * core + q)] = jnp.maximum(total[:coarse], total[coarse:]).astype(jnp.bfloat16)
+    for q in (0, 1):
+        view = enc_ref.at[:, cols(CORES * (1 - core) + q)]
         rcopy(stage.at[q], view, xs.at[6 + q], xr.at[6 + q], partner).wait_recv()
     g.drain()
     for copy in extra + finals:
         copy.wait_send()
 
 
-def encode(w4, prep, edge, skip, chan):
+def encode(filt, prep, edge, skip, chan):
     vm = pl.BlockSpec(memory_space=pltpu.VMEM)
     dma = pltpu.SemaphoreType.DMA
-    quarters, rows, width = w4.shape
+    rows, model_dim = filt.shape
+    width = model_dim // 4
     coarse = prep.shape[1]
     kdepth = SIDE * SIDE * rows // 5
     return pl.pallas_call(
         conv_kernel,
-        out_shape=jax.ShapeDtypeStruct((quarters, coarse, width), jnp.bfloat16),
+        out_shape=jax.ShapeDtypeStruct((coarse, model_dim), jnp.bfloat16),
         in_specs=[vm] * 5,
         out_specs=vm,
         scratch_shapes=[
             pltpu.VMEM((2, 2, SIDE * SIDE, rows, width), jnp.bfloat16),
             pltpu.VMEM((2, 2, 6, coarse, kdepth), jnp.bfloat16),
             pltpu.VMEM(prep.shape, jnp.bfloat16),
-            pltpu.VMEM((2, 2 * coarse, width), jnp.bfloat16),
+            pltpu.VMEM((2 * coarse, 2 * width), jnp.bfloat16),
             pltpu.VMEM((2, 2, 16, prep.shape[2]), jnp.bfloat16),
             pltpu.VMEM((2, 4 * coarse, width), jnp.float32),
             pltpu.VMEM((2, coarse, width), jnp.bfloat16),
         ] + gather_sems() + [dma((8,)), dma((8,))],
         compiler_params=pltpu.CompilerParams(collective_id=0, has_side_effects=True, vmem_limit_bytes=60 << 20),
         name="encode",
-    )(w4, prep, edge, skip, chan)
-
-
-def share_kernel(src_ref, out_ref, zs, zr, ss, rs, ls):
+    )(filt, prep, edge, skip, chan)
+
+
+def share_kernel(src_ref, pair_ref, out_ref, turn_ref, zs, zr, ss, rs, ls, ts, tr):
     rows = src_ref.shape[1]
     g = Gather(out_ref, lambda q: src_ref.at[q], rows, rows // 2, zs, zr, ss, rs, ls)
-    greet(g.peers())
+    n = pair_ref.shape[0]
+    place = g.seq * 2 + g.mp
+    others = [(place + d) % n for d in range(1, n)]
+    devices = [{"seq": p // 2, "mp": p % 2} for p in others]
+    greet(devices)
     g.start_z()
+    turns = [rcopy(pair_ref.at[p], turn_ref.at[place], ts.at[d], tr.at[place], devices[d]) for d, p in enumerate(others)]
+    waiting = list(turns)
+    turn_ref[place] = pair_ref[place]
     for zsel, st in ORDER + [(0, 8), (1, 8)]:
         for q in (0, 1):
             g.stage(q, zsel, st)
+        for copy in waiting[:2]:
+            copy.start()
+        waiting = waiting[2:]
+    for d, p in enumerate(others):
+        view = turn_ref.at[p]
+        rcopy(view, view, ts.at[d], tr.at[p], devices[d]).wait_recv()
     for local in g.pending_local:
         local.wait()
     g.drain()
-
-
-def share(src):
+    for copy in turns:
+        copy.wait_send()
+
+
+def share(src, pair):
     vm = pl.BlockSpec(memory_space=pltpu.VMEM)
+    dma = pltpu.SemaphoreType.DMA
     return pl.pallas_call(
         share_kernel,
-        out_shape=jax.ShapeDtypeStruct((2, 2, SIDE * SIDE) + src.shape[1:], src.dtype),
-        in_specs=[vm],
-        out_specs=vm,
-        scratch_shapes=gather_sems(),
+        out_shape=(
+            jax.ShapeDtypeStruct((2, 2, SIDE * SIDE) + src.shape[1:], src.dtype),
+            jax.ShapeDtypeStruct(pair.shape, pair.dtype),
+        ),
+        in_specs=[vm, vm],
+        out_specs=(vm, vm),
+        scratch_shapes=gather_sems() + [dma((pair.shape[0],))] * 2,
         compiler_params=pltpu.CompilerParams(collective_id=1, has_side_effects=True, vmem_limit_bytes=32 << 20),
         name="share",
-    )(src)
+    )(src, pair)
 
 
 def total_kernel(g_ref, out_ref, R1, R2, fin, s1, r1, s2, r2, s3, r3):
@@ -386,22 +410,20 @@
     pair_dim = flip_weight.shape[0]
     taps, per_shard = conv_weight.shape[:2]
     padded = 48
-    quarter = model_dim // 4
-
-    w4 = jnp.pad(conv_weight, ((0, 0), (0, padded - per_shard), (0, 0)))
-    w4 = w4.reshape(taps * padded, 4, quarter).transpose(1, 0, 2)
+
+    filt = jnp.pad(conv_weight, ((0, 0), (0, padded - per_shard), (0, 0))).reshape(taps * padded, model_dim)
     prepared = prepare(features[0])
     edge = jnp.stack([prepared[:16], prepared[fine_rows - 16 :]])
-    prep = prepared.reshape(coarse, 2, in_channels).transpose(1, 0, 2)
-    skip = jnp.pad(features[0], ((0, 0), (0, model_dim - in_channels)))
-    skip = skip.reshape(coarse, 2, 4, quarter).transpose(2, 1, 0, 3).reshape(4, fine_rows, quarter)
+    wanted = np.arange(fine_rows).reshape(coarse, 2).T.reshape(-1)
+    split = (jnp.asarray(wanted.astype(np.int32))[:, None] == lax.broadcasted_iota(jnp.int32, (1, fine_rows), 1)).astype(jnp.bfloat16)
+    prep = jnp.dot(split, prepared, preferred_element_type=jnp.float32).astype(jnp.bfloat16)
+    prep = prep.reshape(2, coarse, in_channels)
+    skip = jnp.dot(split, features[0], preferred_element_type=jnp.float32).astype(jnp.bfloat16)
+    skip = jnp.pad(skip, ((0, 0), (0, model_dim - in_channels)))
     lane = np.arange(2 * SIDE * SIDE * padded)
     zh, sq, ch = lane // (SIDE * SIDE * padded), (lane // padded) % (SIDE * SIDE), lane % padded
     chan = np.where(ch < per_shard, per_shard * (2 * sq + zh) + ch, -1).astype(np.int32)[None]
-    enc4 = encode(w4, prep, edge, skip, jnp.asarray(chan))
-    encoded = enc4.transpose(1, 0, 2).reshape(coarse, model_dim)
-
-    turned_in = lax.all_to_all(pair_input, ("seq", "mp"), split_axis=2, concat_axis=1, tiled=True)[0]
+    encoded = encode(filt, prep, edge, skip, jnp.asarray(chan))
 
     widened = encoded.astype(jnp.float32)
     normed = (root_norm(widened) * norm_gain).astype(jnp.bfloat16)
@@ -411,7 +433,10 @@
     pair_rows = feats.shape[0]
     spare = jnp.pad(feats.reshape(-1, 64), ((0, coarse - feats.size // 64), (0, 0)))
     block = jnp.concatenate([keyvals, spare], axis=1).reshape(2, coarse // 2, -1)
-    shared = share(block)
+    blocks = 2 * SIDE * SIDE
+    pieces = pair_input[0].reshape(pair_rows, blocks, -1, pair_dim).transpose(1, 0, 2, 3)
+    shared, turned_in = share(block, pieces.reshape(blocks, -1, pair_dim))
+    turned_in = turned_in.reshape(blocks * pair_rows, -1, pair_dim)
     scale_row = jnp.repeat(head_scale, key_dim) / math.sqrt(key_dim)
     queries = (jnp.dot(normed, query_weight, preferred_element_type=jnp.float32) * scale_row).astype(jnp.bfloat16)
 

time: 242 us -> 213 us (0.88)
  local copies, waits for them, and re-layouts: 39.5 us -> 20.2 us
  starting transfers between devices: 14.6 us -> 0 us
  Pallas kernels: 140 us -> 153 us
  other arithmetic: 18.4 us -> 6.78 us
  matrix products: 27.7 us -> 31.4 us
    all_to_all x1 -> x0, starting transfers between devices: 14.6 us -> none  [per_device(): lax.all_to_all(pair_input, ('seq', 'mp'), split_axis=2, concat_axis=1, ti...]
    convert_element_type x5 -> x0, local copies, waits for them, and re-layouts: 12.4 us -> none  [the longest x4 9.47 us: per_device(): widened = encoded.astype(jnp.float32)]
    pallas_call x2, Pallas kernels: 119 us -> 130 us  [the longest x1 90.2 us: encode(): pl.pallas_call(conv_kernel, out_shape=jax.ShapeDtypeStruct((coarse, model...]
    reshape x4 -> x1, local copies, waits for them, and re-layouts: 9.27 us -> 1.23 us  [per_device(): shared, turned_in = share(block, pieces.reshape(blocks, -1, pair_dim))]
    convert_element_type x5 -> x1, other arithmetic: 4.63 us -> 0.01 us  [per_device(): feats[:, pair_dim:].astype(jnp.float32)]
    transpose x1 -> x0, other arithmetic: 4.09 us -> none  [per_device(): prep = prepared.reshape(coarse, 2, in_channels).transpose(1, 0, 2)]
    pallas_call x1, Pallas kernels: 20.6 us -> 23.8 us  [total(): pl.pallas_call(total_kernel, out_shape=jax.ShapeDtypeStruct(term.shape, t...]
    unnamed x32 -> x37, local copies, waits for them, and re-layouts: 5.5 us -> 3.75 us
  transfers between devices with their start and end apart: 1 -> 0, of which waited for: 0 -> 0; matrix products, arithmetic and copies ran while one was open for 32% -> 0% of each run, Pallas kernels for 49% -> 0%
where the time goes in v2:
time: 213 us
  Pallas kernels  153 us (72%)
  matrix products  31.4 us (15%)
  local copies, waits for them, and re-layouts  20.2 us (9%)
  other arithmetic  6.78 us (3%)
    pallas_call x1, Pallas kernels, encode(): pl.pallas_call(conv_kernel, out_shape=jax.ShapeDtypeStruct((coarse, model...  90.2 us
    pallas_call x1, Pallas kernels, share(): pl.pallas_call(share_kernel, out_shape=(jax.ShapeDtypeStruct((2, 2, SIDE...  39.5 us
    pallas_call x1, Pallas kernels, total(): pl.pallas_call(total_kernel, out_shape=jax.ShapeDtypeStruct(term.shape, t...  23.8 us
    dot_general x1, matrix products, per_device(): jnp.dot(weights.astype(jnp.bfloat16), value_rows, preferred_element_type=...  9.52 us
    dot_general x1, matrix products, per_device(): scores = jnp.dot(query_rows, key_rows.T, preferred_element_type=jnp.float32)  9.31 us

profile of v2, /device:TPU:1, one launch (start us, length us, event | category | flops | bytes accessed | tf_op | source)
XLA Modules:
  0.0 212.8 jit_solution(10420068966333187849)
XLA Ops:
  0.7 2.2 %pad.12 = bf16[5,48,1536]{2,1,0:T(8,128)(2,1)} pad(bf16[5,44,1536]{2,1,0:T(8,128)(2,1)} %param.14, bf16[]{:T(256)} %constant.40.clone.1), padding=0_0x0_4x0_0 | pad | bytes 1413122 | tf_op jit(solution)/shard_map/jit(_pad)/pad | solution.py:414
  3.1 3.4 %fusion.10 = bf16[256,1408]{1,0:T(8,128)(2,1)S(1)} fusion(bf16[1,256,1408]{2,1,0:T(8,128)(2,1)S(1)} %copy-done.8, f32[256]{0:T(256)S(1)} %add_rsqrt_fusion), kind=kLoop, calls=%fused_computation.16 | loop fusion | flops 24150016 | bytes 1442816 | tf_op jit(solution)/shard_map/convert_element_type | solution.py:26
  6.6 1.3 convolution_convert_fusion.1
  7.9 0.7 pad_maximum_fusion.edge_ref
  8.5 0.4 convolution_convert_fusion
  8.9 0.9 pad.13.skip_ref
  9.9 90.2 %encode.1 = bf16[128,1536]{1,0:T(8,128)(2,1)} custom-call(bf16[240,1536]{1,0:T(8,128)(2,1)} %bitcast.67, bf16[2,128,1408]{2,1,0:T(8,128)(2,1)} %bitcast.68, bf16[2,16,1408]{2,1,0:T(8,128)(2,1)} %pad_maximum_fusion.edge_ref, bf16[256,1536]{1,0:T(8,128)(2,1)} %pad.13.skip_ref, s32[1,1536]{1,0:T(1,128)} %constant.88.clone.chan_ref), custom_call_target="tpu_custom_call" | custom-call | tf_op jit(solution)/shard_map/encode/pallas_call | solution.py:274
  100.1 1.2 bitcast_reduce_fusion
  101.3 1.3 convolution_convert_fusion.3
  102.6 0.6 copy-done.11
  103.2 0.7 reshape.78
  103.9 0.8 copy.21
  104.9 1.7 convolution_convert_fusion.2
  106.8 1.2 copy_bitcast_fusion.pair_ref
  108.0 39.5 %share.1 = (bf16[2,2,16,64,384]{4,3,2,1,0:T(8,128)(2,1)S(1)}, bf16[32,64,128]{2,1,0:T(8,128)(2,1)S(1)}) custom-call(bf16[2,64,384]{2,1,0:T(8,128)(2,1)S(1)} %bitcast.64, bf16[32,64,128]{2,1,0:T(8,128)(2,1)S(1)} %copy_bitcast_fusion.pair_ref), custom_call_target="tpu_custom_call" | custom-call | tf_op jit(solution)/shard_map/share/pallas_call | solution.py:324
  147.6 0.8 copy-done.1
  148.4 1.6 copy-done.2
  150.1 0.6 fusion.42
  150.7 0.8 reshape.76
  151.6 9.3 %fusion = (f32[1024]{0:T(1024)S(1)}, f32[1024,4096]{1,0:T(8,128)}) fusion(bf16[1024,128]{1,0:T(8,128)(2,1)} %reshape.76, bf16[4096,384]{1,0:T(8,128)(2,1)} %bitcast.65), kind=kOutput, calls=%fused_computation.1 | convolution fusion | flops 1086323712 | bytes 18092032 | tf_op jit(solution)/shard_map/dot_general | solution.py:457
  160.9 9.5 %fusion.51 = bf16[1024,192]{0,1:T(8,128)(2,1)} fusion(bf16[4096,384]{1,0:T(8,128)(2,1)S(1)} %bitcast.66, f32[1024,4096]{1,0:T(8,128)} %get-tuple-element.14, f32[1024]{0:T(1024)S(1)} %get-tuple-element.13), kind=kOutput, calls=%fused_computation.60 | convolution fusion | flops 1623588864 | bytes 19271680 | tf_op jit(solution)/shard_map/dot_general | solution.py:460
  170.4 2.0 copy.24
  172.4 2.3 %reshape.82 = bf16[128,1536]{1,0:T(8,128)(2,1)} reshape(bf16[1024,192]{1,0:T(8,128)(2,1)} %copy.24) | data formatting | bytes 786432 | tf_op jit(solution)/shard_map/reshape | solution.py:461
  174.7 4.0 %fusion.5 = bf16[1,128,1536]{2,1,0:T(8,128)(2,1)} fusion(bf16[128,1536]{1,0:T(8,128)(2,1)} %reshape.82, bf16[1536,1536]{1,0:T(8,128)(2,1)} %param.19, bf16[128,1536]{1,0:T(8,128)(2,1)S(1)} %copy-done.6), kind=kOutput, calls=%fused_computation.8 | convolution fusion | flops 604569600 | bytes 5898240 | tf_op jit(solution)/shard_map/dot_general | solution.py:462
  178.7 1.1 convert_bitcast_fusion
  179.8 0.8 copy.25
  180.7 1.2 reshape.84
  181.9 0.7 fusion.67
  182.6 2.5 %copy.27 = f32[256,8,128]{0,2,1:T(8,128)} copy(bf16[256,8,128]{2,1,0:T(8,128)(2,1)} %bitcast.63) | data formatting | bytes 1572864 | tf_op jit(solution)/shard_map/convert_element_type | solution.py:448
  185.1 2.8 %fusion.41 = bf16[1,8,256,128]{3,2,1,0:T(8,128)(2,1)} fusion(bf16[1,8,256,128]{3,2,1,0:T(8,128)(2,1)} %param.21, f32[256,128]{1,0:T(8,128)S(1)} %get-tuple-element.10, f32[8,128]{1,0:T(8,128)S(1)} %get-tuple-element.12, f32[256,8,128]{0,2,1:T(8,128)} %copy.27, f32[8,128]{1,0:T(8,128)S(1)} %get-tuple-element.11, f32[256,128]{0,1:T(8,128)S(1)} %copy.26, ...), kind=kOutput, calls=%fused_computation.49 | convolution fusion | flops 69730304 | bytes 2400256 | tf_op jit(solution)/shard_map/bac,cd->abd/dot_general | solution.py:449
  188.3 23.8 %total.1 = f32[128,128]{1,0:T(8,128)S(1)} custom-call(f32[128,128]{1,0:T(8,128)S(1)} %convolution_bitcast_fusion.1.g_ref), custom_call_target="tpu_custom_call" | custom-call | tf_op jit(solution)/shard_map/total/pallas_call | solution.py:388
  212.1 0.6 copy.32
  (45 shorter events, 1.1 us)
Async XLA Ops:
  0.6 149.5 %copy-start = (bf16[1536,1024]{1,0:T(8,128)(2,1)S(1)}, bf16[1536,1024]{1,0:T(8,128)(2,1)}, u32[]{:S(2)}) copy-start(bf16[1536,1024]{1,0:T(8,128)(2,1)} %param.16) | copy-start | bytes 9437188
  0.6 2.2 %copy-start.8 = (bf16[1,256,1408]{2,1,0:T(8,128)(2,1)S(1)}, bf16[1,256,1408]{2,1,0:T(8,128)(2,1)}, u32[]{:S(2)}) copy-start(bf16[1,256,1408]{2,1,0:T(8,128)(2,1)} %param.13) | copy-start | bytes 2162692
  2.9 3.7 %copy-start.14 = (s32[256]{0:T(256)S(1)}, s32[256]{0:T(256)}, u32[]{:S(2)}) copy-start(s32[256]{0:T(256)} %constant.87.clone) | copy-start | bytes 3076
  100.1 4.6 %copy-start.4 = (bf16[128,1536]{1,0:T(8,128)(2,1)S(1)}, bf16[128,1536]{1,0:T(8,128)(2,1)}, u32[]{:S(2)}) copy-start(bf16[128,1536]{1,0:T(8,128)(2,1)} %encode.1) | copy-start | bytes 1179652
  102.6 0.6 copy-start.11
  104.9 1.7 copy-start.15
  106.6 43.4 %copy-start.17 = (f32[8]{0:T(128)S(1)}, f32[8]{0:T(128)}, u32[]{:S(2)}) copy-start(f32[8]{0:T(128)} %param.18) | copy-start | bytes 100
  106.6 43.5 %copy-start.13 = (f32[1536]{0:T(1024)S(1)}, f32[1536]{0:T(1024)}, u32[]{:S(2)}) copy-start(f32[1536]{0:T(1024)} %param.15) | copy-start | bytes 18436
  106.7 43.4 %copy-start.16 = (f32[128]{0:T(128)S(1)}, f32[128]{0:T(128)}, u32[]{:S(2)}) copy-start(f32[128]{0:T(128)} %copy-done.15) | copy-start | bytes 1540
  106.8 43.3 %copy-start.5 = (bf16[128,1536]{1,0:T(8,128)(2,1)S(1)}, bf16[128,1536]{1,0:T(8,128)(2,1)}, u32[]{:S(2)}) copy-start(bf16[128,1536]{1,0:T(8,128)(2,1)} %encode.1) | copy-start | bytes 1179652
  147.6 0.8 copy-start.1
  148.4 1.6 copy-start.2
  151.6 9.3 %copy-start.3 = (bf16[2,2,16,64,384]{4,3,2,1,0:T(8,128)(2,1)S(1)}, bf16[2,2,16,64,384]{4,3,2,1,0:T(8,128)(2,1)}, u32[]{:S(2)}) copy-start(bf16[2,2,16,64,384]{4,3,2,1,0:T(8,128)(2,1)} %copy-done.2) | copy-start | bytes 9437188
  170.4 4.3 %copy-start.6 = (bf16[128,1536]{1,0:T(8,128)(2,1)S(1)}, bf16[128,1536]{1,0:T(8,128)(2,1)}, u32[]{:S(2)}) copy-start(bf16[128,1536]{1,0:T(8,128)(2,1)} %encode.1) | copy-start | bytes 1179652
  178.7 3.8 %copy-start.12 = (bf16[8,256]{1,0:T(8,128)(2,1)S(1)}, bf16[8,256]{1,0:T(8,128)(2,1)}, u32[]{:S(2)}) copy-start(bf16[8,256]{1,0:T(8,128)(2,1)} %copy-done.11) | copy-start | bytes 12292
  182.5 2.5 %copy-start.10 = (f32[256,128]{1,0:T(8,128)S(1)}, f32[256,128]{1,0:T(8,128)}, u32[]{:S(2)}) copy-start(f32[256,128]{1,0:T(8,128)} %get-tuple-element.9) | copy-start | bytes 393220
  185.1 2.9 %copy-start.7 = (f32[256,8,128]{0,2,1:T(8,128)S(1)}, f32[256,8,128]{0,2,1:T(8,128)}, u32[]{:S(2)}) copy-start(f32[256,8,128]{0,2,1:T(8,128)} %copy.27) | copy-start | bytes 3145732
  185.1 2.9 %copy-start.9 = (bf16[1,8,256,128]{3,2,1,0:T(8,128)(2,1)S(1)}, bf16[1,8,256,128]{3,2,1,0:T(8,128)(2,1)}, u32[]{:S(2)}) copy-start(bf16[1,8,256,128]{3,2,1,0:T(8,128)(2,1)} %param.23) | copy-start | bytes 1572868

commit v3 on v2

--- a/solution.py
+++ b/solution.py
@@ -335,8 +335,28 @@
     )(src, pair)
 
 
-def total_kernel(g_ref, out_ref, R1, R2, fin, s1, r1, s2, r2, s3, r3):
+def attend_kernel(g_ref, q_ref, kv_ref, out_ref, mix_ref, R1, R2, fin, s1, r1, s2, r2, s3, r3, key_dim, value_dim):
     dp, seq, mp = (lax.axis_index(a) for a in ("dp", "seq", "mp"))
+
+    def attend(first, end):
+        def two(p, carry):
+            mixes = []
+            for e in (0, 1):
+                query = q_ref[:, pl.ds(pl.multiple_of((2 * p + e) * key_dim, key_dim), key_dim)]
+                mixed, norm = 0.0, 0.0
+                for c in range(4):
+                    keys = kv_ref[c // 2, c % 2, :, :, :key_dim].reshape(-1, key_dim)
+                    values = kv_ref[c // 2, c % 2, :, :, key_dim : key_dim + value_dim].reshape(-1, value_dim)
+                    score = lax.dot_general(query, keys, (((1,), (1,)), ((), ())), preferred_element_type=jnp.float32)
+                    weight = jnp.exp(logit_cap * jnp.tanh(score * (1.0 / logit_cap)))
+                    norm += jnp.sum(weight, axis=-1, keepdims=True)
+                    mixed += jnp.dot(weight.astype(jnp.bfloat16), values, preferred_element_type=jnp.float32)
+                mixes.append(mixed / norm)
+            both = jnp.concatenate(mixes, axis=1).astype(jnp.bfloat16)
+            mix_ref[:, pl.ds(pl.multiple_of(p * 2 * value_dim, 2 * value_dim), 2 * value_dim)] = both
+            return carry
+        lax.fori_loop(first, end, two, 0)
+
     n1, n2 = SIDE * SIDE, Z_LO * CORES * 2
     rows = g_ref.shape[0] // n1
     plane = [{"seq": (seq + d) % n1} for d in range(1, n1)]
@@ -353,6 +373,7 @@
         sent.append(c)
     own = g_ref[pl.ds(pl.multiple_of(seq * rows, rows), rows)]
     R1[seq] = own
+    attend(0, 1)
     for d, dev in enumerate(plane):
         view = R1.at[dev["seq"]]
         rcopy(view, view, s1.at[d], r1.at[dev["seq"]], dev).wait_recv()
@@ -362,6 +383,7 @@
         c.start()
         sent.append(c)
     R2[mine] = fin[0]
+    attend(1, 2)
     for d, dev in enumerate(column):
         t = dev["dp"] * 2 + dev["mp"]
         rcopy(R2.at[t], R2.at[t], s2.at[d], r2.at[t], dev).wait_recv()
@@ -372,6 +394,7 @@
         c.start()
         sent.append(c)
     out_ref[piece] = fin[1]
+    attend(2, q_ref.shape[1] // key_dim // 2)
     for d, dev in enumerate(plane):
         view = out_ref.at[pl.ds(pl.multiple_of(dev["seq"] * rows, rows), rows)]
         rcopy(view, view, s3.at[d], r3.at[dev["seq"]], dev).wait_recv()
@@ -379,22 +402,23 @@
         c.wait_send()
 
 
-def total(term):
+def attend_and_total(term, queries, shared, key_dim, value_dim):
     vm = pl.BlockSpec(memory_space=pltpu.VMEM)
     dma = pltpu.SemaphoreType.DMA
     rows = term.shape[0] // (SIDE * SIDE)
     n = SIDE * SIDE
     block = (n, rows, term.shape[1])
+    mixed = (queries.shape[0], queries.shape[1] // key_dim * value_dim)
     return pl.pallas_call(
-        total_kernel,
-        out_shape=jax.ShapeDtypeStruct(term.shape, term.dtype),
-        in_specs=[vm],
-        out_specs=vm,
+        functools.partial(attend_kernel, key_dim=key_dim, value_dim=value_dim),
+        out_shape=(jax.ShapeDtypeStruct(term.shape, term.dtype), jax.ShapeDtypeStruct(mixed, jnp.bfloat16)),
+        in_specs=[vm] * 3,
+        out_specs=(vm, vm),
         scratch_shapes=[pltpu.VMEM(block, jnp.float32), pltpu.VMEM(block, jnp.float32), pltpu.VMEM((2,) + block[1:], jnp.float32)]
         + [dma((n,))] * 6,
-        compiler_params=pltpu.CompilerParams(collective_id=2, has_side_effects=True, vmem_limit_bytes=16 << 20),
-        name="total",
-    )(term)
+        compiler_params=pltpu.CompilerParams(collective_id=2, has_side_effects=True, vmem_limit_bytes=40 << 20),
+        name="attend",
+    )(term, queries, shared)
 
 
 def per_device(
@@ -404,8 +428,7 @@
     fine_rows, in_channels = features.shape[1:]
     coarse = fine_rows // 2
     model_dim = output_weight.shape[1]
-    head_count = head_scale.shape[0]
-    key_dim = query_weight.shape[1] // head_count
+    key_dim = query_weight.shape[1] // head_scale.shape[0]
     value_dim = keyval_weight.shape[1] - key_dim
     pair_dim = flip_weight.shape[0]
     taps, per_shard = conv_weight.shape[:2]
@@ -449,16 +472,8 @@
     turned = jnp.einsum("bac,cd->abd", flipped, flip_weight, preferred_element_type=jnp.float32)
     pair_out = (summed.astype(jnp.float32) + turned).astype(jnp.bfloat16)
     grad_term = jnp.einsum("bac,abd->cd", flipped, pair_cotangent[0], preferred_element_type=jnp.float32)
-    grad_flip = total(grad_term)
-
-    flat = shared.reshape(-1, shared.shape[-1])
-    key_rows, value_rows = flat[:, :key_dim], flat[:, key_dim : key_dim + value_dim]
-    query_rows = queries.reshape(coarse * head_count, key_dim)
-    scores = jnp.dot(query_rows, key_rows.T, preferred_element_type=jnp.float32)
-    weights = jnp.exp(logit_cap * jnp.tanh(scores / logit_cap))
-    totals = jnp.sum(weights, axis=-1, keepdims=True)
-    mixed = jnp.dot(weights.astype(jnp.bfloat16), value_rows, preferred_element_type=jnp.float32) / totals
-    heads_out = mixed.astype(jnp.bfloat16).reshape(coarse, head_count * value_dim)
+    grad_flip, heads_out = attend_and_total(grad_term, queries, shared, key_dim, value_dim)
+
     block_out = (widened + jnp.dot(heads_out, output_weight, preferred_element_type=jnp.float32)).astype(jnp.bfloat16)
     return (block_out[None], pair_out[None], grad_flip)
 

time: 213 us -> 184 us (0.86)
  matrix products: 31.4 us -> 9.84 us
  local copies, waits for them, and re-layouts: 20.2 us -> 10.2 us
  other arithmetic: 6.78 us -> 9.33 us
    dot_general x2 -> x0, matrix products: 18.8 us -> none  [the longest x1 9.52 us: per_device(): jnp.dot(weights.astype(jnp.bfloat16), value_rows, preferred_element_type=...]
    convert_element_type x2 -> x0, local copies, waits for them, and re-layouts: 4.5 us -> none  [the longest x1 2.45 us: per_device(): turned_in.astype(jnp.float32) + q_all[:, None, :] * pair_k[None]]
    reshape x2 -> x0, local copies, waits for them, and re-layouts: 3.08 us -> none  [the longest x1 2.26 us: per_device(): mixed.astype(jnp.bfloat16).reshape(coarse, head_count * value_dim)]
    reduce_sum x2, other arithmetic: 0.38 us -> 2.73 us  [root_norm(): jnp.mean(values_in * values_in, axis=-1, keepdims=True) + norm_eps]
    unnamed x37 -> x31, local copies, waits for them, and re-layouts: 3.75 us -> 4.68 us
where the time goes in v3:
time: 184 us; the launch traced here: 183 us
  Pallas kernels  153 us (83%)
  local copies, waits for them, and re-layouts  10.2 us (6%)
  matrix products  9.84 us (5%)
  other arithmetic  9.33 us (5%)
    pallas_call x1, Pallas kernels, encode(): pl.pallas_call(conv_kernel, out_shape=jax.ShapeDtypeStruct((coarse, model...  90.2 us
    pallas_call x1, Pallas kernels, share(): pl.pallas_call(share_kernel, out_shape=(jax.ShapeDtypeStruct((2, 2, SIDE...  39.5 us
    pallas_call x1, Pallas kernels, attend_and_total(): pl.pallas_call(functools.partial(attend_kernel, key_dim=key_dim, value_di...  23.4 us
    unnamed x31, local copies, waits for them, and re-layouts  4.68 us
    convert_element_type x1, other arithmetic, prepare(): jax.nn.gelu(root_norm(raw.astype(jnp.float32)), approximate=False)  4.47 us
    dot_general x1, matrix products, per_device(): jnp.dot(heads_out, output_weight, preferred_element_type=jnp.float32)  3.87 us

profile of v3, /device:TPU:1, one launch (start us, length us, event | category | flops | bytes accessed | tf_op | source)
XLA Modules:
  0.0 183.5 jit_solution(15909810490110486429)
XLA Ops:
  0.7 1.5 fusion.33
  2.2 4.5 %fusion.5 = bf16[256,1408]{1,0:T(8,128)(2,1)S(1)} fusion(bf16[1,256,1408]{2,1,0:T(8,128)(2,1)} %param.13, f32[256]{0:T(256)S(1)} %add_rsqrt_fusion), kind=kLoop, calls=%fused_computation.11 | loop fusion | flops 24150016 | bytes 1442816 | tf_op jit(solution)/shard_map/convert_element_type | solution.py:26
  6.7 0.7 pad_maximum_fusion.edge_ref
  7.3 1.3 convolution_convert_fusion.1
  8.6 0.4 convolution_convert_fusion
  9.0 0.9 pad.13.skip_ref
  10.0 0.9 pad.12
  10.9 90.2 %encode.1 = bf16[128,1536]{1,0:T(8,128)(2,1)} custom-call(bf16[240,1536]{1,0:T(8,128)(2,1)} %bitcast.63, bf16[2,128,1408]{2,1,0:T(8,128)(2,1)} %bitcast.64, bf16[2,16,1408]{2,1,0:T(8,128)(2,1)} %pad_maximum_fusion.edge_ref, bf16[256,1536]{1,0:T(8,128)(2,1)} %pad.13.skip_ref, s32[1,1536]{1,0:T(1,128)} %constant.84.clone.chan_ref), custom_call_target="tpu_custom_call" | custom-call | tf_op jit(solution)/shard_map/encode/pallas_call | solution.py:274
  101.2 1.2 multiply_reduce_fusion
  102.4 1.8 convolution_convert_fusion.2
  104.3 0.1 bitcast_reduce_fusion
  104.4 0.2 convolution_convert_fusion.3
  104.6 0.1 reshape.67
  104.7 0.1 copy.20
  104.8 0.1 copy.21
  105.0 1.2 copy_bitcast_fusion.pair_ref
  106.1 39.5 %share.1 = (bf16[2,2,16,64,384]{4,3,2,1,0:T(8,128)(2,1)S(1)}, bf16[32,64,128]{2,1,0:T(8,128)(2,1)S(1)}) custom-call(bf16[2,64,384]{2,1,0:T(8,128)(2,1)S(1)} %bitcast.62, bf16[32,64,128]{2,1,0:T(8,128)(2,1)S(1)} %copy_bitcast_fusion.pair_ref), custom_call_target="tpu_custom_call" | custom-call | tf_op jit(solution)/shard_map/share/pallas_call | solution.py:324
  145.7 0.1 convert_bitcast_fusion
  145.8 0.6 copy-done.3
  146.5 1.6 copy-done.1
  148.1 0.9 copy.23
  149.0 1.2 reshape.71
  150.2 1.2 convert.5
  151.4 1.2 fusion.36
  152.6 0.5 convolution_bitcast_fusion.1.g_ref
  153.1 0.2 copy-done.14
  153.3 0.3 copy-done.5
  153.6 0.6 fusion.37.q_ref
  154.2 1.3 copy-done.2
  155.5 23.4 %attend.1 = (f32[128,128]{1,0:T(8,128)S(1)}, bf16[128,1536]{1,0:T(8,128)(2,1)S(1)}) custom-call(f32[128,128]{1,0:T(8,128)S(1)} %convolution_bitcast_fusion.1.g_ref, bf16[128,1024]{1,0:T(8,128)(2,1)S(1)} %fusion.37.q_ref, bf16[2,2,16,64,384]{4,3,2,1,0:T(8,128)(2,1)S(1)} %copy-done.2), custom_call_target="tpu_custom_call" | custom-call | tf_op jit(solution)/shard_map/attend/pallas_call | solution.py:412
  179.0 3.9 %fusion.1 = bf16[1,128,1536]{2,1,0:T(8,128)(2,1)} fusion(bf16[128,1536]{1,0:T(8,128)(2,1)S(1)} %get-tuple-element.9, bf16[1536,1536]{1,0:T(8,128)(2,1)} %param.19, bf16[128,1536]{1,0:T(8,128)(2,1)S(1)} %copy-done.5), kind=kOutput, calls=%fused_computation.4 | convolution fusion | flops 604569600 | bytes 5898240 | tf_op jit(solution)/shard_map/dot_general | solution.py:477
  182.8 0.6 copy.34
  (33 shorter events, 0.2 us)
Async XLA Ops:
  0.6 152.7 %copy-start = (bf16[1536,1024]{1,0:T(8,128)(2,1)S(1)}, bf16[1536,1024]{1,0:T(8,128)(2,1)}, u32[]{:S(2)}) copy-start(bf16[1536,1024]{1,0:T(8,128)(2,1)} %param.16) | copy-start | bytes 9437188
  0.6 6.7 %copy-start.13 = (s32[256]{0:T(256)S(1)}, s32[256]{0:T(256)}, u32[]{:S(2)}) copy-start(s32[256]{0:T(256)} %constant.83.clone) | copy-start | bytes 3076
  2.2 6.5 %copy-start.6 = (bf16[1,256,1408]{2,1,0:T(8,128)(2,1)S(1)}, bf16[1,256,1408]{2,1,0:T(8,128)(2,1)}, u32[]{:S(2)}) copy-start(bf16[1,256,1408]{2,1,0:T(8,128)(2,1)} %param.13) | copy-start | bytes 2162692
  8.6 1.4 copy-start.9
  10.9 91.5 %copy-start.12 = (f32[1536]{0:T(1024)S(1)}, f32[1536]{0:T(1024)}, u32[]{:S(2)}) copy-start(f32[1536]{0:T(1024)} %param.15) | copy-start | bytes 18436
  101.1 3.1 %copy-start.4 = (bf16[128,1536]{1,0:T(8,128)(2,1)S(1)}, bf16[128,1536]{1,0:T(8,128)(2,1)}, u32[]{:S(2)}) copy-start(bf16[128,1536]{1,0:T(8,128)(2,1)} %encode.1) | copy-start | bytes 1179652
  101.1 3.2 %copy-start.8 = (bf16[1536,256]{1,0:T(8,128)(2,1)S(1)}, bf16[1536,256]{1,0:T(8,128)(2,1)}, u32[]{:S(2)}) copy-start(bf16[1536,256]{1,0:T(8,128)(2,1)} %param.20) | copy-start | bytes 2359300
  145.7 0.8 copy-start.3
  146.5 1.6 copy-start.1
  149.0 2.5 %copy-start.11 = (bf16[128,128]{1,0:T(8,128)(2,1)S(1)}, bf16[128,128]{1,0:T(8,128)(2,1)}, u32[]{:S(2)}) copy-start(bf16[128,128]{1,0:T(8,128)(2,1)} %param.22) | copy-start | bytes 98308
  150.2 1.2 copy-start.7
  151.4 1.2 copy-start.10
  152.6 0.7 copy-start.14
  152.6 1.0 copy-start.5
  153.6 1.9 %copy-start.2 = (bf16[2,2,16,64,384]{4,3,2,1,0:T(8,128)(2,1)S(1)}, bf16[2,2,16,64,384]{4,3,2,1,0:T(8,128)(2,1)}, u32[]{:S(2)}) copy-start(bf16[2,2,16,64,384]{4,3,2,1,0:T(8,128)(2,1)} %copy-done.1) | copy-start | bytes 9437188

commit v4 on v3

--- a/solution.py
+++ b/solution.py
@@ -227,9 +227,9 @@
     for local in g.pending_local:
         local.wait()
 
-    def conv(zsel):
+    def conv(zsel, colours):
         za = g.z_of(zsel)
-        for q in (0, 1):
+        for q in colours:
             def tap(k, carry):
                 lhs = X[:, za, pl.ds(k, 2)].reshape(acc.shape[1], -1)
                 rhs = F[q, za, :, pl.ds(pl.multiple_of(k * depth, 16), depth), :].reshape(-1, width)
@@ -240,14 +240,14 @@
     acc[...] = jnp.zeros_like(acc)
     for q in (0, 1):
         g.stage(q, 0, 8)
-    conv(0)
+    conv(0, (0, 1))
     for q in (0, 1):
         g.stage(q, 1, 8)
-    conv(1)
     half = acc.shape[1] // 2
     coarse = half // 2
     finals = []
     for q in (0, 1):
+        conv(1, (q,))
         total = acc[q, half:] + S2[:, q * width : (q + 1) * width].astype(jnp.float32)
         stage[q] = jnp.maximum(total[:coarse], total[coarse:]).astype(jnp.bfloat16)
         copy = rcopy(stage.at[q], enc_ref.at[:, cols(CORES * core + q)], xs.at[6 + q], xr.at[6 + q], partner)

time: 184 us -> 184 us (level)
  no operation moved by 1% of the time
where the time goes in v4:
time: 184 us; the launch traced here: 183 us
  Pallas kernels  153 us (83%)
  local copies, waits for them, and re-layouts  10.2 us (6%)
  matrix products  9.84 us (5%)
  other arithmetic  9.33 us (5%)
    pallas_call x1, Pallas kernels, encode(): pl.pallas_call(conv_kernel, out_shape=jax.ShapeDtypeStruct((coarse, model...  90.1 us
    pallas_call x1, Pallas kernels, share(): pl.pallas_call(share_kernel, out_shape=(jax.ShapeDtypeStruct((2, 2, SIDE...  39.5 us
    pallas_call x1, Pallas kernels, attend_and_total(): pl.pallas_call(functools.partial(attend_kernel, key_dim=key_dim, value_di...  23.5 us
    unnamed x31, local copies, waits for them, and re-layouts  4.68 us
    convert_element_type x1, other arithmetic, prepare(): jax.nn.gelu(root_norm(raw.astype(jnp.float32)), approximate=False)  4.47 us
    dot_general x1, matrix products, per_device(): jnp.dot(heads_out, output_weight, preferred_element_type=jnp.float32)  3.87 us

profile of v4, /device:TPU:1, one launch (start us, length us, event | category | flops | bytes accessed | tf_op | source)
XLA Modules:
  0.0 183.4 jit_solution(14275511817340123393)
XLA Ops:
  0.7 1.5 fusion.33
  2.2 4.5 %fusion.5 = bf16[256,1408]{1,0:T(8,128)(2,1)S(1)} fusion(bf16[1,256,1408]{2,1,0:T(8,128)(2,1)} %param.13, f32[256]{0:T(256)S(1)} %add_rsqrt_fusion), kind=kLoop, calls=%fused_computation.11 | loop fusion | flops 24150016 | bytes 1442816 | tf_op jit(solution)/shard_map/convert_element_type | solution.py:26
  6.7 0.7 pad_maximum_fusion.edge_ref
  7.3 1.3 convolution_convert_fusion.1
  8.6 0.4 convolution_convert_fusion
  9.0 0.9 pad.13.skip_ref
  10.0 0.9 pad.12
  10.9 90.1 %encode.1 = bf16[128,1536]{1,0:T(8,128)(2,1)} custom-call(bf16[240,1536]{1,0:T(8,128)(2,1)} %bitcast.63, bf16[2,128,1408]{2,1,0:T(8,128)(2,1)} %bitcast.64, bf16[2,16,1408]{2,1,0:T(8,128)(2,1)} %pad_maximum_fusion.edge_ref, bf16[256,1536]{1,0:T(8,128)(2,1)} %pad.13.skip_ref, s32[1,1536]{1,0:T(1,128)} %constant.84.clone.chan_ref), custom_call_target="tpu_custom_call" | custom-call | tf_op jit(solution)/shard_map/encode/pallas_call | solution.py:274
  101.1 1.2 multiply_reduce_fusion
  102.3 1.8 convolution_convert_fusion.2
  104.1 0.1 bitcast_reduce_fusion
  104.3 0.2 convolution_convert_fusion.3
  104.5 0.1 reshape.67
  104.6 0.1 copy.20
  104.7 0.1 copy.21
  104.9 1.2 copy_bitcast_fusion.pair_ref
  106.0 39.5 %share.1 = (bf16[2,2,16,64,384]{4,3,2,1,0:T(8,128)(2,1)S(1)}, bf16[32,64,128]{2,1,0:T(8,128)(2,1)S(1)}) custom-call(bf16[2,64,384]{2,1,0:T(8,128)(2,1)S(1)} %bitcast.62, bf16[32,64,128]{2,1,0:T(8,128)(2,1)S(1)} %copy_bitcast_fusion.pair_ref), custom_call_target="tpu_custom_call" | custom-call | tf_op jit(solution)/shard_map/share/pallas_call | solution.py:324
  145.6 0.1 convert_bitcast_fusion
  145.7 0.6 copy-done.3
  146.4 1.6 copy-done.1
  148.0 0.9 copy.23
  148.9 1.2 reshape.71
  150.1 1.2 convert.5
  151.3 1.2 fusion.36
  152.5 0.5 convolution_bitcast_fusion.1.g_ref
  153.0 0.2 copy-done.14
  153.2 0.3 copy-done.5
  153.5 0.6 fusion.37.q_ref
  154.1 1.3 copy-done.2
  155.4 23.5 %attend.1 = (f32[128,128]{1,0:T(8,128)S(1)}, bf16[128,1536]{1,0:T(8,128)(2,1)S(1)}) custom-call(f32[128,128]{1,0:T(8,128)S(1)} %convolution_bitcast_fusion.1.g_ref, bf16[128,1024]{1,0:T(8,128)(2,1)S(1)} %fusion.37.q_ref, bf16[2,2,16,64,384]{4,3,2,1,0:T(8,128)(2,1)S(1)} %copy-done.2), custom_call_target="tpu_custom_call" | custom-call | tf_op jit(solution)/shard_map/attend/pallas_call | solution.py:412
  178.9 3.9 %fusion.1 = bf16[1,128,1536]{2,1,0:T(8,128)(2,1)} fusion(bf16[128,1536]{1,0:T(8,128)(2,1)S(1)} %get-tuple-element.9, bf16[1536,1536]{1,0:T(8,128)(2,1)} %param.19, bf16[128,1536]{1,0:T(8,128)(2,1)S(1)} %copy-done.5), kind=kOutput, calls=%fused_computation.4 | convolution fusion | flops 604569600 | bytes 5898240 | tf_op jit(solution)/shard_map/dot_general | solution.py:477
  182.8 0.6 copy.34
  (33 shorter events, 0.2 us)
Async XLA Ops:
  0.6 152.6 %copy-start = (bf16[1536,1024]{1,0:T(8,128)(2,1)S(1)}, bf16[1536,1024]{1,0:T(8,128)(2,1)}, u32[]{:S(2)}) copy-start(bf16[1536,1024]{1,0:T(8,128)(2,1)} %param.16) | copy-start | bytes 9437188
  0.6 6.7 %copy-start.13 = (s32[256]{0:T(256)S(1)}, s32[256]{0:T(256)}, u32[]{:S(2)}) copy-start(s32[256]{0:T(256)} %constant.83.clone) | copy-start | bytes 3076
  2.2 6.5 %copy-start.6 = (bf16[1,256,1408]{2,1,0:T(8,128)(2,1)S(1)}, bf16[1,256,1408]{2,1,0:T(8,128)(2,1)}, u32[]{:S(2)}) copy-start(bf16[1,256,1408]{2,1,0:T(8,128)(2,1)} %param.13) | copy-start | bytes 2162692
  8.6 1.4 copy-start.9
  10.9 91.4 %copy-start.12 = (f32[1536]{0:T(1024)S(1)}, f32[1536]{0:T(1024)}, u32[]{:S(2)}) copy-start(f32[1536]{0:T(1024)} %param.15) | copy-start | bytes 18436
  101.0 3.1 %copy-start.4 = (bf16[128,1536]{1,0:T(8,128)(2,1)S(1)}, bf16[128,1536]{1,0:T(8,128)(2,1)}, u32[]{:S(2)}) copy-start(bf16[128,1536]{1,0:T(8,128)(2,1)} %encode.1) | copy-start | bytes 1179652
  101.0 3.2 %copy-start.8 = (bf16[1536,256]{1,0:T(8,128)(2,1)S(1)}, bf16[1536,256]{1,0:T(8,128)(2,1)}, u32[]{:S(2)}) copy-start(bf16[1536,256]{1,0:T(8,128)(2,1)} %param.20) | copy-start | bytes 2359300
  145.6 0.8 copy-start.3
  146.4 1.6 copy-start.1
  148.9 2.5 %copy-start.11 = (bf16[128,128]{1,0:T(8,128)(2,1)S(1)}, bf16[128,128]{1,0:T(8,128)(2,1)}, u32[]{:S(2)}) copy-start(bf16[128,128]{1,0:T(8,128)(2,1)} %param.22) | copy-start | bytes 98308
  150.1 1.2 copy-start.7
  151.3 1.2 copy-start.10
  152.5 0.7 copy-start.14
  152.5 1.0 copy-start.5
  153.5 1.9 %copy-start.2 = (bf16[2,2,16,64,384]{4,3,2,1,0:T(8,128)(2,1)S(1)}, bf16[2,2,16,64,384]{4,3,2,1,0:T(8,128)(2,1)}, u32[]{:S(2)}) copy-start(bf16[2,2,16,64,384]{4,3,2,1,0:T(8,128)(2,1)} %copy-done.1) | copy-start | bytes 9437188
